TPU v7x, 32 devices: a whole 2x2x4 slice. The times are simulated.
32 devices in a mesh: gx: 2 (over core), gy: 4 (over y, x), gz: 4 (over z).
Axes of the slice: x: 2, y: 2, z: 4, core: 2. Of those that a mesh axis runs over, the one named last changes fastest.
Arguments:
- offsets: float32 [3, 4, 8, 8, 128], P(None, 'gx', 'gy', 'gz'), may hold values from 0 to 1
- velocity: float32 [3, 4, 8, 8, 128], P(None, 'gx', 'gy', 'gz'), may hold values from -6 to 6
- mass: float32 [4, 8, 8, 128], P('gx', 'gy', 'gz'), may hold values from 0.005 to 0.02
- counts: int32 [4, 8, 8], P('gx', 'gy', 'gz'), may hold values from 1 to 128
Outputs:
- accel: float32 [3, 4, 8, 8, 128], P(None, 'gx', 'gy', 'gz')
- density: float32 [4, 8, 8, 128], P('gx', 'gy', 'gz')
Inputs may be any that keep to these rules, and one draw needn't show every extreme that they name: `counts`: slots of a cell at or beyond its count are empty.
All inputs are finite; a program needn't handle non-finite values.
Results may differ from a plain program's by a relative error of at most 0.0003.
Values sent between devices are 32-bit elements; how exact they have to be, the bound alone decides.
No kernel may reach another device: no remote copies, remote signals or barrier semaphores. Data moves between devices by JAX's collectives and lax.ppermute only.
A program may use at most 64 MiB of HBM per device.

v0:
```python
import functools
import math

import jax
import jax.numpy as jnp
from jax import lax
from jax.experimental import pallas as pl
from jax.experimental.pallas import tpu as pltpu
from jax.sharding import PartitionSpec as P

KERNEL_NORM = 315.0 / (64.0 * math.pi)
PRESSURE_COEF = 0.5
SUB = 8


def partner_pairs(sizes, axis, kind):
    n, nx = sizes[axis], sizes["gx"]
    pairs = []
    for i in range(n):
        j = (i ^ 1) if kind == "A" else ((i - 1) ^ 1) + 1
        if i == 0 and kind == "B" or j >= n or j < 0:
            j = i
        pairs.append(j)
    if axis == "gx":
        if kind == "B":
            pairs[0], pairs[n - 1] = n - 1, 0
        return "gx", [(i, j) for i, j in enumerate(pairs)]
    if all(i != j for i, j in enumerate(pairs)):
        return axis, list(enumerate(pairs))
    out = []
    for x in range(nx):
        for i, j in enumerate(pairs):
            to = (x, j)
            if i == j and nx % 2 == 0:
                to = (x ^ 1, j)
            out.append((x * n + i, to[0] * n + to[1]))
    return ("gx", axis), out


def swap(message, sizes, axis, kind):
    names, pairs = partner_pairs(sizes, axis, kind)
    return lax.ppermute(message, names, pairs)


def kinds_of(n):
    return ("A", "B") if n > 2 else ("A",) if n > 1 else ()


def extend(cells, sizes, axis, dim):
    size = cells.shape[dim]
    parts = [cells]
    for kind in kinds_of(sizes[axis]):
        at = size - 1 if kind == "A" else 0
        parts.append(swap(lax.slice_in_dim(cells, at, at + 1, axis=dim), sizes, axis, kind))
    return jnp.concatenate(parts, axis=dim)


def order_of(size, n):
    return list(range(1, size + 1)) + [{"A": size + 1, "B": 0}[k] for k in kinds_of(n)]


class Plan:
    def __init__(self, sizes, extents, slots):
        self.sizes, self.extents, self.slots = sizes, extents, slots
        self.lx, self.ly, self.lz = extents
        self.X = order_of(self.lx, sizes["gx"])
        self.Y = order_of(self.ly, sizes["gy"])
        self.columns = len(self.X) * len(self.Y)
        self.cells = self.columns * self.lz
        self.own_columns = [(x, y) for x in range(1, self.lx + 1) for y in range(1, self.ly + 1)]
        self.own_cells = [(x, y, z) for x, y in self.own_columns for z in range(1, self.lz + 1)]
        self.owns = len(self.own_cells)

    def column_index(self, x, y):
        return self.X.index(x) * len(self.Y) + self.Y.index(y)

    def cell_index(self, x, y, z):
        return self.column_index(x, y) * self.lz + z - 1

    def near_columns(self, x, y):
        return [
            self.column_index(x + a, y + b)
            for a in (-1, 0, 1)
            for b in (-1, 0, 1)
            if x + a in self.X and y + b in self.Y
        ]

    def near_cells(self, x, y, z):
        return [k * self.lz + c - 1 for k in self.near_columns(x, y) for c in (z - 1, z, z + 1) if 1 <= c <= self.lz]

    def near_sides(self, x, y, z):
        sides = [side for side in range(2) if z == (self.lz if side == 0 else 1)]
        return [side * self.columns + k for side in sides for k in self.near_columns(x, y)]


GROUPS_J = (0, 0, 1, 1, 0, 2)
GROUPS_I = (0, 1, 0, 1, 2, 0)
DEPTH = 32
ROWS = 16
BF16 = jnp.bfloat16
F32 = jnp.float32


def split3(x):
    high = x.astype(BF16).astype(F32)
    rest = x - high
    middle = rest.astype(BF16).astype(F32)
    return high, middle, rest - middle


def dot(a, b):
    return jnp.dot(a, b, preferred_element_type=F32)


def groups_of(rows):
    return [(a, min(SUB, rows - a)) for a in range(0, rows, SUB)]


def put_features(out, values, order, first, count):
    parts = [split3(v) for v in values]
    for group, which in enumerate(order):
        for r, part in enumerate(parts):
            out[pl.ds(first * DEPTH + group * len(values) + r, count, stride=DEPTH), :] = part[which]
    zero = jnp.zeros_like(values[0])
    for r in range(len(order) * len(values), DEPTH):
        out[pl.ds(first * DEPTH + r, count, stride=DEPTH), :] = zero


def near_features(x, y, z, g):
    return [g * (1.0 - (x * x + y * y + z * z)), -g, 2.0 * g * x, 2.0 * g * y, 2.0 * g * z]


AXES = ("gx", "gy", "gz")


class Places:
    def __init__(self, plan):
        self.mirrored, self.shift, self.inside = [], [], []
        for k, axis in enumerate(AXES):
            extent, n = plan.extents[k], plan.sizes[axis]
            i = lax.axis_index(axis)
            odd = lax.rem(i, 2) == 1
            self.mirrored.append(odd)
            sign = jnp.where(odd, -1.0, 1.0).astype(F32)
            self.shift.append([sign * (p - 0.5 * (extent + 1)) - 0.5 for p in range(extent + 2)])
            above = jnp.where(jnp.where(odd, i - 1, i + 1) < n, 1.0, 0.0).astype(F32)
            below = jnp.where(odd, jnp.where(i + 1 < n, 1.0, 0.0), jnp.where(i > 0, 1.0, 0.0)).astype(F32)
            self.inside.append([below] + [jnp.float32(1.0)] * extent + [above])

    def source(self, plan, cell):
        at = jnp.int32(0)
        for k in range(3):
            i, extent = cell[k] - 1, plan.extents[k]
            at = at * extent + jnp.where(self.mirrored[k], extent - 1 - i, i)
        return at


def pattern(values, period, slots):
    at = lax.broadcasted_iota(jnp.int32, (len(values) * period, slots), 0)
    out = jnp.full(at.shape, values[0])
    for r in range(1, len(values)):
        out = jnp.where(at >= r * period, values[r], out)
    return out


def place_cells(plan, places, ref, out, xs, ys, zs):
    slots, rows = plan.slots, len(ys) * len(zs)
    cells = rows * len(xs)
    shift_y = pattern([places.shift[1][y] for y in ys], len(zs), slots)
    keep_y = pattern([places.inside[1][y] for y in ys], len(zs), slots)
    if len(zs) == 1:
        shift_z, keep_z = places.shift[2][zs[0]], places.inside[2][zs[0]]
    else:
        at = lax.rem(lax.broadcasted_iota(jnp.int32, (rows, slots), 0), len(zs))
        shift_z, keep_z = jnp.full(at.shape, places.shift[2][zs[0]]), 1.0
        for r in range(1, len(zs)):
            shift_z = jnp.where(at == r, places.shift[2][zs[r]], shift_z)
    keep_yz = keep_y * keep_z
    for g, x in enumerate(xs):
        at = [pl.ds(f * cells + g * rows, rows) for f in range(4)]
        out[at[0], :] = ref[at[0], :] + places.shift[0][x]
        out[at[1], :] = ref[at[1], :] + shift_y
        out[at[2], :] = ref[at[2], :] + shift_z
        out[at[3], :] = ref[at[3], :] * (keep_yz * places.inside[0][x])


def own_range(plan, k):
    return list(range(1, plan.extents[k] + 1))


def numbers_of(state, plan):
    full = jnp.where(state[pl.ds(3 * plan.owns, plan.owns), :] > 0.0, 1.0, 0.0)
    return [jnp.sum(full[o : o + 1, :]).astype(jnp.int32) for o in range(plan.owns)]


def near_operand(staged, left, ref, cells, first):
    slots = ref.shape[1]
    for start, count in groups_of(cells):
        values = near_features(*(ref[pl.ds(f * cells + start, count), :] for f in range(4)))
        put_features(staged, values, GROUPS_J, first + start, count)
    for c in range(first, first + cells):
        left[pl.ds(c * slots, slots), :] = staged[pl.ds(c * DEPTH, DEPTH), :].T.astype(BF16)


def prepare_kernel(plan, fields, state, speed):
    owns, slots = plan.owns, plan.slots
    places = Places(plan)
    for o, cell in enumerate(plan.own_cells):
        at = places.source(plan, cell)
        for f in range(3):
            state[pl.ds(f * owns + o, 1), :] = fields[pl.ds(f * owns + at, 1), :]
        speed[pl.ds(3 * owns + o, 1), :] = fields[pl.ds(7 * owns + at, 1), :]
        state[pl.ds(3 * owns + o, 1), :] = fields[pl.ds(6 * owns + at, 1), :]
    heavy = state[pl.ds(3 * owns, owns), :] * KERNEL_NORM
    root = jnp.exp(jnp.log(heavy) * (1.0 / 3.0))
    root = root * (2.0 / 3.0) + heavy / (3.0 * root * root)
    lane = lax.broadcasted_iota(jnp.int32, (owns, slots), 1).astype(F32)
    state[pl.ds(3 * owns, owns), :] = jnp.where(lane < speed[pl.ds(3 * owns, owns), :], root, 0.0)
    for o, cell in enumerate(plan.own_cells):
        at = places.source(plan, cell)
        for f in range(3):
            speed[pl.ds(f * owns + o, 1), :] = fields[pl.ds((3 + f) * owns + at, 1), :] * (1.0 / 6.0)


def cubes(left, right):
    q = jnp.maximum(dot(left, right), 0.0)
    return jnp.sum((q * q * q).reshape(q.shape[0] // SUB, SUB, q.shape[1]), axis=0)


def density_block_kernel(plan, raw, cells, right, sums, staged, own, left):
    slots = plan.slots
    place_cells(plan, Places(plan), raw, cells, plan.X, plan.Y, own_range(plan, 2))
    near_operand(staged, left, cells, plan.cells, 0)
    for p, (x, y) in enumerate(plan.own_columns):
        for z in range(plan.lz):
            c = plan.cell_index(x, y, z + 1)
            line = [cells[pl.ds(f * plan.cells + c, 1), :] for f in range(3)]
            values = [jnp.ones_like(line[0]), line[0] * line[0] + line[1] * line[1] + line[2] * line[2], *line]
            put_features(own, values, GROUPS_I, 0, 1)
            right[p, :, pl.ds(z * slots, slots)] = own[...].astype(BF16)
    for p, (x, y) in enumerate(plan.own_columns):
        mine = right[p]
        total = jnp.zeros((SUB, plan.lz * slots), F32)
        for k in plan.near_columns(x, y):
            total += cubes(left[pl.ds(k * plan.lz * slots, plan.lz * slots), :], mine)
        sums[p] = total


def density_side_kernel(
    plan, raw_a, raw_b, state, speed, right, sums, za, zb, flow, density, staged, left
):
    slots, n, owns = plan.slots, plan.columns, plan.owns
    places = Places(plan)
    for side, (raw, ref) in enumerate(((raw_a, za), (raw_b, zb))):
        place_cells(plan, places, raw, ref, plan.X, plan.Y, [plan.lz + 1 if side == 0 else 0])
        near_operand(staged, left, ref, n, side * n)
    flow[pl.ds(0, 3 * owns), :] = speed[pl.ds(0, 3 * owns), :]
    for o, (x, y, z) in enumerate(plan.own_cells):
        p = plan.own_columns.index((x, y))
        lanes = pl.ds((z - 1) * slots, slots)
        total = sums[p, :, lanes]
        mine = right[p, :, lanes]
        for c in plan.near_sides(x, y, z):
            total += cubes(left[pl.ds(c * slots, slots), :], mine)
        total = jnp.sum(total, axis=0, keepdims=True)
        full = state[pl.ds(3 * owns + o, 1), :] > 0.0
        density[pl.ds(places.source(plan, (x, y, z)), 1), :] = jnp.where(full, total, 0.0)
        flow[pl.ds(3 * owns + o, 1), :] = PRESSURE_COEF / jnp.where(full, total, 1.0)


def force_rows(out, ref, flow, cells, first):
    for start, count in groups_of(cells):
        g = ref[pl.ds(3 * cells + start, count), :]
        m = g * g * g
        out[0, pl.ds(first + start, count), :] = m
        out[1, pl.ds(first + start, count), :] = m * flow[pl.ds(3 * cells + start, count), :]


def line_of(ref, row):
    return ref[pl.ds(row, SUB, stride=0), :]


def force_pairs(count, near, columns, o, start, sums):
    def step(i, carry):
        base = pl.multiple_of(i * ROWS, ROWS)
        at = [pl.ds(base + r, SUB) for r in range(0, ROWS, SUB)]
        own = [[columns[f, o, a, :] for f in range(4)] for a in at]
        total = [[None] * 4 for _ in at] if start is None else [[start[k, o, a, :] for k in range(4)] for a in at]
        add = lambda old, new: new if old is None else old + new
        for lines in near:
            x, y, z, m, c, vx, vy, vz = lines()
            for r in range(len(at)):
                d = [own[r][0] - x, own[r][1] - y, own[r][2] - z]
                q = jnp.maximum(1.0 - (d[0] * d[0] + d[1] * d[1] + d[2] * d[2]), 0.0)
                q2 = q * q
                p = (m * own[r][3] + c) * q2
                w = c * (q2 * q)
                total[r][3] = add(total[r][3], w)
                for f, v in enumerate((vx, vy, vz)):
                    total[r][f] = add(total[r][f], p * d[f] + w * v)
        for r, a in enumerate(at):
            for k in range(4):
                sums[k, o, a, :] = total[r][k]
        return carry

    lax.fori_loop(0, lax.div(count + (ROWS - 1), ROWS), step, 0)


def lines_from(ref, flow, extra, cells, c, e):
    return lambda: (
        *(line_of(ref, f * cells + c) for f in range(3)),
        *(line_of(extra.at[k], e) for k in range(2)),
        *(line_of(flow, f * cells + c) for f in range(3)),
    )


def force_own_kernel(plan, cells, flow, columns, sums, extra, placed):
    slots, owns = plan.slots, plan.owns
    numbers = numbers_of(cells, plan)
    place_cells(plan, Places(plan), cells, placed, *(own_range(plan, k) for k in range(3)))
    rows = [placed[pl.ds(0, 3 * owns), :], flow[pl.ds(3 * owns, owns), :], jnp.zeros((slots - 4 * owns, slots), F32)]
    table = jnp.concatenate(rows, axis=0).T
    for f in range(4):
        for o in range(owns):
            e = f * owns + o
            columns[f, o] = jnp.broadcast_to(table[:, e : e + 1], (slots, slots))
    force_rows(extra, placed, flow, owns, 0)
    for o, cell in enumerate(plan.own_cells):
        near = [
            lines_from(placed, flow, extra, owns, c, c)
            for c, other in enumerate(plan.own_cells)
            if max(abs(p - q) for p, q in zip(cell, other)) <= 1
        ]
        force_pairs(numbers[o], near, columns, o, None, sums)


def force_block_kernel(plan, state, cells, flow, columns, start, sums, extra):
    numbers = numbers_of(state, plan)
    force_rows(extra, cells, flow, plan.cells, 0)
    own = [plan.cell_index(*cell) for cell in plan.own_cells]
    for o, (x, y, z) in enumerate(plan.own_cells):
        near = [
            lines_from(cells, flow, extra, plan.cells, c, c) for c in plan.near_cells(x, y, z) if c not in own
        ]
        force_pairs(numbers[o], near, columns, o, start, sums)


def force_side_kernel(plan, state, flow, za, zb, fza, fzb, columns, start, accel, sums, extra):
    slots, n, owns = plan.slots, plan.columns, plan.owns
    numbers = numbers_of(state, plan)
    places = Places(plan)
    for side, (ref, fref) in enumerate(((za, fza), (zb, fzb))):
        force_rows(extra, ref, fref, n, side * n)
    for o, (x, y, z) in enumerate(plan.own_cells):
        near = []
        for e in plan.near_sides(x, y, z):
            side, k = divmod(e, n)
            near.append(lines_from((za, zb)[side], (fza, fzb)[side], extra, n, k, e))
        force_pairs(numbers[o], near, columns, o, start, sums)
    lane = lax.broadcasted_iota(jnp.int32, (slots, slots), 1)
    table = jnp.zeros((slots, slots), F32)
    for e in range(4 * owns):
        table = jnp.where(lane == e, jnp.sum(sums[e // owns, e % owns], axis=1, keepdims=True), table)
    whole = table.T
    for o, cell in enumerate(plan.own_cells):
        at = places.source(plan, cell)
        full = state[pl.ds(3 * owns + o, 1), :] > 0.0
        for f in range(3):
            v = flow[pl.ds(f * owns + o, 1), :]
            value = 6.0 * (whole[f * owns + o : f * owns + o + 1] - v * whole[3 * owns + o : 3 * owns + o + 1])
            accel[pl.ds(f * owns + at, 1), :] = jnp.where(full, value, 0.0)


def call(kernel, args, outs, scratch, cost, aliases=None):
    vmem = pl.BlockSpec(memory_space=pltpu.VMEM)
    return pl.pallas_call(
        kernel,
        out_shape=[jax.ShapeDtypeStruct(shape, dtype) for shape, dtype in outs],
        in_specs=[vmem] * len(args),
        out_specs=[vmem] * len(outs),
        scratch_shapes=scratch,
        input_output_aliases=aliases or {},
        cost_estimate=pl.CostEstimate(flops=cost, bytes_accessed=1 << 20, transcendentals=0),
        compiler_params=pltpu.CompilerParams(vmem_limit_bytes=16 << 20),
    )(*args)


def local(sizes, offsets, velocity, mass, counts):
    slots = offsets.shape[-1]
    extents = offsets.shape[1:4]
    plan = Plan(sizes, extents, slots)
    pairs, lz, total, columns, owns = len(plan.own_columns), plan.lz, plan.cells, plan.columns, plan.owns
    flat = lambda cells: cells.reshape(-1, slots)

    def gather(state):
        block = extend(state.reshape((4,) + extents + (slots,)), sizes, "gx", 1)
        block = extend(block, sizes, "gy", 2)
        sides = []
        for kind in ("A", "B"):
            at = lz - 1 if kind == "A" else 0
            message = lax.slice_in_dim(block, at, at + 1, axis=3)
            present = kind in kinds_of(sizes["gz"])
            sides.append(flat(swap(message, sizes, "gz", kind) if present else jnp.zeros_like(message)))
        return flat(block), sides

    number = jnp.broadcast_to(counts.astype(F32)[..., None], mass.shape)
    fields = flat(jnp.concatenate([offsets, velocity, mass[None], number[None]], axis=0))
    state, speed = call(
        functools.partial(prepare_kernel, plan),
        [fields],
        [((4 * owns, slots), F32), ((4 * owns, slots), F32)],
        [],
        1 << 20,
    )
    raw, (raw_a, raw_b) = gather(state)
    cells, right, sums = call(
        functools.partial(density_block_kernel, plan),
        [raw],
        [
            ((4 * total, slots), F32),
            ((pairs, DEPTH, lz * slots), BF16),
            ((pairs, SUB, lz * slots), F32),
        ],
        [
            pltpu.VMEM((total * DEPTH, slots), F32),
            pltpu.VMEM((DEPTH, slots), F32),
            pltpu.VMEM((total * slots, DEPTH), BF16),
        ],
        1 << 27,
    )
    side = ((4 * columns, slots), F32)
    za, zb, flow_state, density = call(
        functools.partial(density_side_kernel, plan),
        [raw_a, raw_b, state, speed, right, sums],
        [side, side, ((4 * owns, slots), F32), ((owns, slots), F32)],
        [pltpu.VMEM((2 * columns * DEPTH, slots), F32), pltpu.VMEM((2 * columns * slots, DEPTH), BF16)],
        1 << 26,
    )
    flow, (fza, fzb) = gather(flow_state)
    wide = (4, owns, slots, slots)
    repeated, partial = call(
        functools.partial(force_own_kernel, plan),
        [state, flow_state],
        [(wide, F32), (wide, F32)],
        [pltpu.VMEM((2, owns, slots), F32), pltpu.VMEM((4 * owns, slots), F32)],
        1 << 27,
    )
    (partial,) = call(
        functools.partial(force_block_kernel, plan),
        [state, cells, flow, repeated, partial],
        [(wide, F32)],
        [pltpu.VMEM((2, total, slots), F32)],
        1 << 27,
        {4: 0},
    )
    (force,) = call(
        functools.partial(force_side_kernel, plan),
        [state, flow_state, za, zb, fza, fzb, repeated, partial],
        [((3 * owns, slots), F32)],
        [pltpu.VMEM(wide, F32), pltpu.VMEM((2, 2 * columns, slots), F32)],
        1 << 27,
    )
    return force.reshape(offsets.shape), density.reshape(mass.shape)


def layer(sizes, *args):
    return local(sizes, *args)


def solution(mesh):
    sizes = dict(mesh.shape)
    in_specs = (
        P(None, "gx", "gy", "gz", None),
        P(None, "gx", "gy", "gz", None),
        P("gx", "gy", "gz", None),
        P("gx", "gy", "gz"),
    )
    out_specs = (P(None, "gx", "gy", "gz", None), P("gx", "gy", "gz", None))
    return jax.shard_map(
        functools.partial(layer, sizes), mesh=mesh, in_specs=in_specs, out_specs=out_specs, check_vma=False
    )
```

profile of v0, /device:TPU:0, one launch (start us, length us, event | category | flops | bytes accessed | tf_op | source)
XLA Modules:
  0.0 34.7 jit_solution(5422314558346867402)
XLA Ops:
  0.6 0.7 %convert_element_type.3 = f32[2,2,2]{2,1,0:T(2,128)S(1)} convert(s32[2,2,2]{2,1,0:T(2,128)} %param.7) | non-fusion elementwise | flops 8 | bytes 64 | tf_op jit(solution)/shard_map/convert_element_type | solution.py:406
  1.3 0.1 broadcast_in_dim_broadcast_in_dim.2
  1.4 0.8 %pad_maximum_fusion.2 = f32[8,2,2,2,128]{4,3,2,1,0:T(2,128)S(1)} fusion(f32[1,2,2,2,128]{4,3,2,1,0:T(2,128)S(1)} %broadcast_in_dim_broadcast_in_dim.2, f32[1,2,2,2,128]{4,3,2,1,0:T(2,128)} %bitcast.24, f32[3,2,2,2,128]{4,3,2,1,0:T(2,128)} %param.5, f32[3,2,2,2,128]{4,3,2,1,0:T(2,128)} %param.4), kind=kLoop, calls=%fused_computation.2 | loop fusion | flops 24576 | bytes 65536 | tf_op jit(solution)/shard_map/concatenate | solution.py:407
  2.1 0.1 shard_map.59
  2.2 0.6 %collective-permute-start = (f32[4,1,2,2,128]{4,2,1,0,3:T(2,128)S(1)}, f32[4,1,2,2,128]{4,2,1,0,3:T(2,128)S(1)}, u32[]{:S(2)}, u32[]{:S(2)}) collective-permute-start(f32[4,1,2,2,128]{4,2,1,0,3:T(2,128)S(1)} %copy.15), channel_id=1, source_target_pairs={{0,16},{16,0},{1,17},{17,1},{2,18},{18,2},{3,19},{19,3},{4,20},{20... | collective-permute-start | bytes 24584 | tf_op jit(solution)/shard_map/ppermute | solution.py:42
  2.8 0.8 %collective-permute-done = f32[4,1,2,2,128]{4,2,1,0,3:T(2,128)S(1)} collective-permute-done((f32[4,1,2,2,128]{4,2,1,0,3:T(2,128)S(1)}, f32[4,1,2,2,128]{4,2,1,0,3:T(2,128)S(1)}, u32[]{:S(2)}, u32[]{:S(2)}) %collective-permute-start) | collective-permute-done | bytes 8224 | tf_op jit(solution)/shard_map/ppermute | solution.py:42
  3.7 2.9 %collective-permute-start.1 = (f32[4,3,1,2,128]{4,2,1,0,3:T(1,128)S(1)}, f32[4,3,1,2,128]{4,2,1,0,3:T(1,128)S(1)}, u32[]{:S(2)}, u32[]{:S(2)}) collective-permute-start(f32[4,3,1,2,128]{4,2,1,0,3:T(1,128)S(1)} %get-tuple-element.30), channel_id=1, source_target_pairs={{0,4},{4,0},{8,12},{12,8},{1,5},{5,1},{9,13},{13,9},{2,6},{6,2},{1... | collective-permute-start | bytes 36872 | tf_op jit(solution)/shard_map/ppermute | solution.py:42
  6.5 0.0 collective-permute-start.2
  6.5 1.7 %collective-permute-done.1 = f32[4,3,1,2,128]{4,2,1,0,3:T(1,128)S(1)} collective-permute-done((f32[4,3,1,2,128]{4,2,1,0,3:T(1,128)S(1)}, f32[4,3,1,2,128]{4,2,1,0,3:T(1,128)S(1)}, u32[]{:S(2)}, u32[]{:S(2)}) %collective-permute-start.1) | collective-permute-done | bytes 12320 | tf_op jit(solution)/shard_map/ppermute | solution.py:42
  8.2 0.0 collective-permute-done.2
  8.3 0.1 collective-permute-start.4
  8.4 3.7 %collective-permute-start.3 = (f32[4,3,4,1,128]{4,2,1,0,3:T(4,128)S(1)}, f32[4,3,4,1,128]{4,2,1,0,3:T(4,128)S(1)}, u32[]{:S(2)}, u32[]{:S(2)}) collective-permute-start(f32[4,3,4,1,128]{4,2,1,0,3:T(4,128)S(1)} %get-tuple-element.27), channel_id=1, source_target_pairs={{0,1},{1,0},{2,3},{3,2},{4,5},{5,4},{6,7},{7,6},{8,9},{9,8},{10,11... | collective-permute-start | bytes 73736 | tf_op jit(solution)/shard_map/ppermute | solution.py:42
  12.1 1.8 %shard_map.60 = (f32[96,128]{1,0:T(8,128)S(1)}, bf16[4,32,256]{2,1,0:T(8,128)(2,1)S(1)}, f32[4,8,256]{2,1,0:T(8,128)S(1)}) custom-call(f32[96,128]{1,0:T(8,128)S(1)} %bitcast.18), custom_call_target="tpu_custom_call" | custom-call | flops 134217728 | bytes 1048576 | tf_op jit(solution)/shard_map/pallas_call | solution.py:376
  13.8 0.0 collective-permute-done.3
  13.8 1.7 %shard_map.61 = (f32[48,128]{1,0:T(8,128)S(1)}, f32[48,128]{1,0:T(8,128)S(1)}, f32[32,128]{1,0:T(8,128)S(1)}, f32[8,128]{1,0:T(8,128)}) custom-call(f32[48,128]{1,0:T(8,128)S(1)} %bitcast.22, f32[48,128]{1,0:T(8,128)S(1)} %bitcast.21, f32[32,128]{1,0:T(8,128)S(1)} %get-tuple-element.13.state.cells, f32[32,128]{1,0:T(8,128)S(1)} %get-tuple-element.14.speed, ...), custom_call_target="tpu_custom_call" | custom-call | flops 67108864 | bytes 1048576 | tf_op jit(solution)/shard_map/pallas_call | solution.py:376
  15.6 0.1 collective-permute-start.5
  15.7 1.1 %collective-permute-done.5 = f32[4,1,2,2,128]{4,2,1,0,3:T(2,128)S(1)} collective-permute-done((f32[4,1,2,2,128]{4,2,1,0,3:T(2,128)S(1)}, f32[4,1,2,2,128]{4,2,1,0,3:T(2,128)S(1)}, u32[]{:S(2)}, u32[]{:S(2)}) %collective-permute-start.5) | collective-permute-done | bytes 8224 | tf_op jit(solution)/shard_map/ppermute | solution.py:42
  16.9 3.0 %collective-permute-start.6 = (f32[4,3,1,2,128]{4,2,1,0,3:T(1,128)S(1)}, f32[4,3,1,2,128]{4,2,1,0,3:T(1,128)S(1)}, u32[]{:S(2)}, u32[]{:S(2)}) collective-permute-start(f32[4,3,1,2,128]{4,2,1,0,3:T(1,128)S(1)} %get-tuple-element.28), channel_id=1, source_target_pairs={{0,4},{4,0},{8,12},{12,8},{1,5},{5,1},{9,13},{13,9},{2,6},{6,2},{1... | collective-permute-start | bytes 36872 | tf_op jit(solution)/shard_map/ppermute | solution.py:42
  19.8 1.7 %collective-permute-done.6 = f32[4,3,1,2,128]{4,2,1,0,3:T(1,128)S(1)} collective-permute-done((f32[4,3,1,2,128]{4,2,1,0,3:T(1,128)S(1)}, f32[4,3,1,2,128]{4,2,1,0,3:T(1,128)S(1)}, u32[]{:S(2)}, u32[]{:S(2)}) %collective-permute-start.6) | collective-permute-done | bytes 12320 | tf_op jit(solution)/shard_map/ppermute | solution.py:42
  21.6 0.1 collective-permute-start.9
  21.7 2.4 %collective-permute-start.8 = (f32[4,3,4,1,128]{4,2,1,0,3:T(4,128)S(1)}, f32[4,3,4,1,128]{4,2,1,0,3:T(4,128)S(1)}, u32[]{:S(2)}, u32[]{:S(2)}) collective-permute-start(f32[4,3,4,1,128]{4,2,1,0,3:T(4,128)S(1)} %get-tuple-element.25), channel_id=1, source_target_pairs={{0,1},{1,0},{2,3},{3,2},{4,5},{5,4},{6,7},{7,6},{8,9},{9,8},{10,11... | collective-permute-start | bytes 73736 | tf_op jit(solution)/shard_map/ppermute | solution.py:42
  24.1 3.7 %shard_map.62 = (f32[4,8,128,128]{3,2,1,0:T(8,128)S(1)}, f32[4,8,128,128]{3,2,1,0:T(8,128)S(1)}) custom-call(f32[32,128]{1,0:T(8,128)S(1)} %get-tuple-element.13.state.cells, f32[32,128]{1,0:T(8,128)S(1)} %get-tuple-element.17.flow), custom_call_target="tpu_custom_call" | custom-call | flops 134217728 | bytes 1048576 | tf_op jit(solution)/shard_map/pallas_call | solution.py:376
  27.8 2.6 %shard_map.63.start = f32[4,8,128,128]{3,2,1,0:T(8,128)S(1)} custom-call(f32[32,128]{1,0:T(8,128)S(1)} %get-tuple-element.13.state.cells, f32[96,128]{1,0:T(8,128)S(1)} %get-tuple-element.21.cells, f32[96,128]{1,0:T(8,128)S(1)} %bitcast.14, f32[4,8,128,128]{3,2,1,0:T(8,128)S(1)} %get-tuple-element.20.columns, ...), custom_call_target="tpu_custom_call", output_to_operand_aliasing={{}: (4, {})} | custom-call | flops 134217728 | bytes 1048576 | tf_op jit(solution)/shard_map/pallas_call | solution.py:376
  30.5 4.2 %shard_map.64 = f32[24,128]{1,0:T(8,128)} custom-call(f32[32,128]{1,0:T(8,128)S(1)} %get-tuple-element.13.state.cells, f32[32,128]{1,0:T(8,128)S(1)} %get-tuple-element.17.flow, f32[48,128]{1,0:T(8,128)S(1)} %get-tuple-element.18.za, f32[48,128]{1,0:T(8,128)S(1)} %get-tuple-element.19.zb, f32[48,128]{1,0:T(8,128)S(1)} %bitcast.20, f32[48,128]{1,0:T(8,128)S(1)} %bitcast.19, ...), custom_call_target="tpu_custom_call" | custom-call | flops 134217728 | bytes 1048576 | tf_op jit(solution)/shard_map/pallas_call | solution.py:376
  (21 shorter events, 0.3 us)
Async XLA Ops:
  2.2 1.4 %collective-permute-start = (f32[4,1,2,2,128]{4,2,1,0,3:T(2,128)S(1)}, f32[4,1,2,2,128]{4,2,1,0,3:T(2,128)S(1)}, u32[]{:S(2)}, u32[]{:S(2)}) collective-permute-start(f32[4,1,2,2,128]{4,2,1,0,3:T(2,128)S(1)} %copy.15), channel_id=1, source_target_pairs={{0,16},{16,0},{1,17},{17,1},{2,18},{18,2},{3,19},{19,3},{4,20},{20... | collective-permute-start | bytes 24584 | tf_op jit(solution)/shard_map/ppermute | solution.py:42
  3.7 4.6 %collective-permute-start.1 = (f32[4,3,1,2,128]{4,2,1,0,3:T(1,128)S(1)}, f32[4,3,1,2,128]{4,2,1,0,3:T(1,128)S(1)}, u32[]{:S(2)}, u32[]{:S(2)}) collective-permute-start(f32[4,3,1,2,128]{4,2,1,0,3:T(1,128)S(1)} %get-tuple-element.30), channel_id=1, source_target_pairs={{0,4},{4,0},{8,12},{12,8},{1,5},{5,1},{9,13},{13,9},{2,6},{6,2},{1... | collective-permute-start | bytes 36872 | tf_op jit(solution)/shard_map/ppermute | solution.py:42
  6.5 1.7 %collective-permute-start.2 = (f32[4,3,1,2,128]{4,2,1,0,3:T(1,128)S(1)}, f32[4,3,1,2,128]{4,2,1,0,3:T(1,128)S(1)}, u32[]{:S(2)}, u32[]{:S(2)}) collective-permute-start(f32[4,3,1,2,128]{4,2,1,0,3:T(1,128)S(1)} %get-tuple-element.31), channel_id=1, source_target_pairs={{0,16},{4,8},{8,4},{12,28},{16,0},{20,24},{24,20},{28,12},{1,17},{... | collective-permute-start | bytes 36872 | tf_op jit(solution)/shard_map/ppermute | solution.py:42
  8.3 5.5 %collective-permute-start.4 = (f32[4,3,4,1,128]{4,2,1,0,3:T(4,128)S(1)}, f32[4,3,4,1,128]{4,2,1,0,3:T(4,128)S(1)}, u32[]{:S(2)}, u32[]{:S(2)}) collective-permute-start(f32[4,3,4,1,128]{4,2,1,0,3:T(4,128)S(1)} %get-tuple-element.26), channel_id=1, source_target_pairs={{0,16},{1,2},{2,1},{3,19},{16,0},{17,18},{18,17},{19,3},{4,20},{5,... | collective-permute-start | bytes 73736 | tf_op jit(solution)/shard_map/ppermute | solution.py:42
  8.4 5.5 %collective-permute-start.3 = (f32[4,3,4,1,128]{4,2,1,0,3:T(4,128)S(1)}, f32[4,3,4,1,128]{4,2,1,0,3:T(4,128)S(1)}, u32[]{:S(2)}, u32[]{:S(2)}) collective-permute-start(f32[4,3,4,1,128]{4,2,1,0,3:T(4,128)S(1)} %get-tuple-element.27), channel_id=1, source_target_pairs={{0,1},{1,0},{2,3},{3,2},{4,5},{5,4},{6,7},{7,6},{8,9},{9,8},{10,11... | collective-permute-start | bytes 73736 | tf_op jit(solution)/shard_map/ppermute | solution.py:42
  15.6 1.2 %collective-permute-start.5 = (f32[4,1,2,2,128]{4,2,1,0,3:T(2,128)S(1)}, f32[4,1,2,2,128]{4,2,1,0,3:T(2,128)S(1)}, u32[]{:S(2)}, u32[]{:S(2)}) collective-permute-start(f32[4,1,2,2,128]{4,2,1,0,3:T(2,128)S(1)} %copy.16), channel_id=1, source_target_pairs={{0,16},{16,0},{1,17},{17,1},{2,18},{18,2},{3,19},{19,3},{4,20},{20... | collective-permute-start | bytes 24584 | tf_op jit(solution)/shard_map/ppermute | solution.py:42
  16.9 4.7 %collective-permute-start.6 = (f32[4,3,1,2,128]{4,2,1,0,3:T(1,128)S(1)}, f32[4,3,1,2,128]{4,2,1,0,3:T(1,128)S(1)}, u32[]{:S(2)}, u32[]{:S(2)}) collective-permute-start(f32[4,3,1,2,128]{4,2,1,0,3:T(1,128)S(1)} %get-tuple-element.28), channel_id=1, source_target_pairs={{0,4},{4,0},{8,12},{12,8},{1,5},{5,1},{9,13},{13,9},{2,6},{6,2},{1... | collective-permute-start | bytes 36872 | tf_op jit(solution)/shard_map/ppermute | solution.py:42
  19.8 1.7 %collective-permute-start.7 = (f32[4,3,1,2,128]{4,2,1,0,3:T(1,128)S(1)}, f32[4,3,1,2,128]{4,2,1,0,3:T(1,128)S(1)}, u32[]{:S(2)}, u32[]{:S(2)}) collective-permute-start(f32[4,3,1,2,128]{4,2,1,0,3:T(1,128)S(1)} %get-tuple-element.29), channel_id=1, source_target_pairs={{0,16},{4,8},{8,4},{12,28},{16,0},{20,24},{24,20},{28,12},{1,17},{... | collective-permute-start | bytes 36872 | tf_op jit(solution)/shard_map/ppermute | solution.py:42
  21.6 8.9 %collective-permute-start.9 = (f32[4,3,4,1,128]{4,2,1,0,3:T(4,128)S(1)}, f32[4,3,4,1,128]{4,2,1,0,3:T(4,128)S(1)}, u32[]{:S(2)}, u32[]{:S(2)}) collective-permute-start(f32[4,3,4,1,128]{4,2,1,0,3:T(4,128)S(1)} %get-tuple-element.24), channel_id=1, source_target_pairs={{0,16},{1,2},{2,1},{3,19},{16,0},{17,18},{18,17},{19,3},{4,20},{5,... | collective-permute-start | bytes 73736 | tf_op jit(solution)/shard_map/ppermute | solution.py:42
  21.7 8.8 %collective-permute-start.8 = (f32[4,3,4,1,128]{4,2,1,0,3:T(4,128)S(1)}, f32[4,3,4,1,128]{4,2,1,0,3:T(4,128)S(1)}, u32[]{:S(2)}, u32[]{:S(2)}) collective-permute-start(f32[4,3,4,1,128]{4,2,1,0,3:T(4,128)S(1)} %get-tuple-element.25), channel_id=1, source_target_pairs={{0,1},{1,0},{2,3},{3,2},{4,5},{5,4},{6,7},{7,6},{8,9},{9,8},{10,11... | collective-permute-start | bytes 73736 | tf_op jit(solution)/shard_map/ppermute | solution.py:42
where the time goes:
time: 34.9 us; the launch traced here: 34.7 us
  Pallas kernels  14.1 us (40%)
  starting transfers between devices  12.8 us (37%)
  waiting for transfers between devices  5.32 us (15%)
  other arithmetic  1.52 us (4%)
  between operations  0.79 us (2%)
    pallas_call x6, Pallas kernels, call(): pl.pallas_call(kernel, out_shape=[jax.ShapeDtypeStruct(shape, dtype) for...  14.1 us
    ppermute x10, starting transfers between devices, swap(): return lax.ppermute(message, names, pairs)  12.8 us
    ppermute x10, waiting for transfers between devices, swap(): return lax.ppermute(message, names, pairs)  5.32 us
    concatenate x1, other arithmetic, local(): jnp.concatenate([offsets, velocity, mass[None], number[None]], axis=0)  0.76 us
  transfers between devices with their start and end apart: 10, of which 4 were waited for; matrix products, arithmetic and copies ran while one was open for 0% of the time, Pallas kernels for 23%

commit v1 on v0

--- a/solution.py
+++ b/solution.py
@@ -88,9 +88,12 @@
     def near_cells(self, x, y, z):
         return [k * self.lz + c - 1 for k in self.near_columns(x, y) for c in (z - 1, z, z + 1) if 1 <= c <= self.lz]
 
-    def near_sides(self, x, y, z):
-        sides = [side for side in range(2) if z == (self.lz if side == 0 else 1)]
-        return [side * self.columns + k for side in sides for k in self.near_columns(x, y)]
+    def beside(self, side):
+        z = self.lz if side == 0 else 1
+        return [(o, cell) for o, cell in enumerate(self.own_cells) if cell[2] == z]
+
+    def lanes(self, cell):
+        return self.own_columns.index(cell[:2]), pl.ds((cell[2] - 1) * self.slots, self.slots)
 
 
 GROUPS_J = (0, 0, 1, 1, 0, 2)
@@ -147,12 +150,12 @@
             below = jnp.where(odd, jnp.where(i + 1 < n, 1.0, 0.0), jnp.where(i > 0, 1.0, 0.0)).astype(F32)
             self.inside.append([below] + [jnp.float32(1.0)] * extent + [above])
 
+    def source_position(self, plan, cell):
+        return [jnp.where(self.mirrored[k], plan.extents[k] - cell[k], cell[k] - 1) for k in range(3)]
+
     def source(self, plan, cell):
-        at = jnp.int32(0)
-        for k in range(3):
-            i, extent = cell[k] - 1, plan.extents[k]
-            at = at * extent + jnp.where(self.mirrored[k], extent - 1 - i, i)
-        return at
+        x, y, z = self.source_position(plan, cell)
+        return (x * plan.extents[1] + y) * plan.extents[2] + z
 
 
 def pattern(values, period, slots):
@@ -202,20 +205,26 @@
         left[pl.ds(c * slots, slots), :] = staged[pl.ds(c * DEPTH, DEPTH), :].T.astype(BF16)
 
 
-def prepare_kernel(plan, fields, state, speed):
+def prepare_kernel(plan, fields, counts, state, speed):
     owns, slots = plan.owns, plan.slots
     places = Places(plan)
+    row = lax.broadcasted_iota(jnp.int32, plan.extents[1:], 0)
+    column = lax.broadcasted_iota(jnp.int32, plan.extents[1:], 1)
+    line = lax.broadcasted_iota(jnp.int32, (owns, slots), 0)
+    held = jnp.zeros((owns, slots), F32)
     for o, cell in enumerate(plan.own_cells):
         at = places.source(plan, cell)
+        x, y, z = places.source_position(plan, cell)
+        number = jnp.sum(jnp.where((row == y) & (column == z), counts[x].astype(F32), 0.0))
+        held = jnp.where(line == o, number, held)
         for f in range(3):
             state[pl.ds(f * owns + o, 1), :] = fields[pl.ds(f * owns + at, 1), :]
-        speed[pl.ds(3 * owns + o, 1), :] = fields[pl.ds(7 * owns + at, 1), :]
         state[pl.ds(3 * owns + o, 1), :] = fields[pl.ds(6 * owns + at, 1), :]
     heavy = state[pl.ds(3 * owns, owns), :] * KERNEL_NORM
     root = jnp.exp(jnp.log(heavy) * (1.0 / 3.0))
     root = root * (2.0 / 3.0) + heavy / (3.0 * root * root)
     lane = lax.broadcasted_iota(jnp.int32, (owns, slots), 1).astype(F32)
-    state[pl.ds(3 * owns, owns), :] = jnp.where(lane < speed[pl.ds(3 * owns, owns), :], root, 0.0)
+    state[pl.ds(3 * owns, owns), :] = jnp.where(lane < held, root, 0.0)
     for o, cell in enumerate(plan.own_cells):
         at = places.source(plan, cell)
         for f in range(3):
@@ -246,129 +255,199 @@
         sums[p] = total
 
 
-def density_side_kernel(
-    plan, raw_a, raw_b, state, speed, right, sums, za, zb, flow, density, staged, left
-):
-    slots, n, owns = plan.slots, plan.columns, plan.owns
+def density_side(plan, side, raw, placed, right, sums, staged, left):
+    slots = plan.slots
     places = Places(plan)
-    for side, (raw, ref) in enumerate(((raw_a, za), (raw_b, zb))):
-        place_cells(plan, places, raw, ref, plan.X, plan.Y, [plan.lz + 1 if side == 0 else 0])
-        near_operand(staged, left, ref, n, side * n)
-    flow[pl.ds(0, 3 * owns), :] = speed[pl.ds(0, 3 * owns), :]
-    for o, (x, y, z) in enumerate(plan.own_cells):
-        p = plan.own_columns.index((x, y))
-        lanes = pl.ds((z - 1) * slots, slots)
+    place_cells(plan, places, raw, placed, plan.X, plan.Y, [plan.lz + 1 if side == 0 else 0])
+    near_operand(staged, left, placed, plan.columns, 0)
+    out = {}
+    for o, cell in plan.beside(side):
+        p, lanes = plan.lanes(cell)
         total = sums[p, :, lanes]
         mine = right[p, :, lanes]
-        for c in plan.near_sides(x, y, z):
-            total += cubes(left[pl.ds(c * slots, slots), :], mine)
-        total = jnp.sum(total, axis=0, keepdims=True)
-        full = state[pl.ds(3 * owns + o, 1), :] > 0.0
-        density[pl.ds(places.source(plan, (x, y, z)), 1), :] = jnp.where(full, total, 0.0)
-        flow[pl.ds(3 * owns + o, 1), :] = PRESSURE_COEF / jnp.where(full, total, 1.0)
-
-
-def force_rows(out, ref, flow, cells, first):
+        for k in plan.near_columns(*cell[:2]):
+            total += cubes(left[pl.ds(k * slots, slots), :], mine)
+        out[o] = total
+    return out
+
+
+def density_above_kernel(plan, raw, right, sums, placed, out, staged, left):
+    done = density_side(plan, 0, raw, placed, right, sums, staged, left)
+    for o, cell in enumerate(plan.own_cells):
+        p, lanes = plan.lanes(cell)
+        out[p, :, lanes] = done[o] if o in done else sums[p, :, lanes]
+
+
+def density_below_kernel(plan, raw, state, speed, right, sums, placed, flow, density, staged, left):
+    owns = plan.owns
+    done = density_side(plan, 1, raw, placed, right, sums, staged, left)
+    rows = []
+    for o, cell in enumerate(plan.own_cells):
+        p, lanes = plan.lanes(cell)
+        rows.append(jnp.sum(done[o] if o in done else sums[p, :, lanes], axis=0, keepdims=True))
+    total = jnp.concatenate(rows, axis=0)
+    full = state[pl.ds(3 * owns, owns), :] > 0.0
+    flow[pl.ds(0, 3 * owns), :] = speed[...]
+    flow[pl.ds(3 * owns, owns), :] = PRESSURE_COEF / jnp.where(full, total, 1.0)
+    density[...] = jnp.where(full, total, 0.0)
+
+
+def gather_fields(out, near, flow, cells):
     for start, count in groups_of(cells):
-        g = ref[pl.ds(3 * cells + start, count), :]
+        rows = [pl.ds(f * cells + start, count) for f in range(8)]
+        g = near[rows[3], :]
         m = g * g * g
-        out[0, pl.ds(first + start, count), :] = m
-        out[1, pl.ds(first + start, count), :] = m * flow[pl.ds(3 * cells + start, count), :]
-
-
-def line_of(ref, row):
-    return ref[pl.ds(row, SUB, stride=0), :]
-
-
-def force_pairs(count, near, columns, o, start, sums):
-    def step(i, carry):
-        base = pl.multiple_of(i * ROWS, ROWS)
-        at = [pl.ds(base + r, SUB) for r in range(0, ROWS, SUB)]
-        own = [[columns[f, o, a, :] for f in range(4)] for a in at]
-        total = [[None] * 4 for _ in at] if start is None else [[start[k, o, a, :] for k in range(4)] for a in at]
-        add = lambda old, new: new if old is None else old + new
-        for lines in near:
-            x, y, z, m, c, vx, vy, vz = lines()
-            for r in range(len(at)):
-                d = [own[r][0] - x, own[r][1] - y, own[r][2] - z]
-                q = jnp.maximum(1.0 - (d[0] * d[0] + d[1] * d[1] + d[2] * d[2]), 0.0)
-                q2 = q * q
-                p = (m * own[r][3] + c) * q2
-                w = c * (q2 * q)
-                total[r][3] = add(total[r][3], w)
-                for f, v in enumerate((vx, vy, vz)):
-                    total[r][f] = add(total[r][f], p * d[f] + w * v)
-        for r, a in enumerate(at):
-            for k in range(4):
-                sums[k, o, a, :] = total[r][k]
-        return carry
-
-    lax.fori_loop(0, lax.div(count + (ROWS - 1), ROWS), step, 0)
-
-
-def lines_from(ref, flow, extra, cells, c, e):
-    return lambda: (
-        *(line_of(ref, f * cells + c) for f in range(3)),
-        *(line_of(extra.at[k], e) for k in range(2)),
-        *(line_of(flow, f * cells + c) for f in range(3)),
-    )
-
-
-def force_own_kernel(plan, cells, flow, columns, sums, extra, placed):
-    slots, owns = plan.slots, plan.owns
-    numbers = numbers_of(cells, plan)
+        for f in range(3):
+            out[rows[f], :] = near[rows[f], :]
+            out[rows[5 + f], :] = flow[rows[f], :]
+        out[rows[3], :] = m
+        out[rows[4], :] = m * flow[rows[3], :]
+
+
+def pack(plan, fields, cells, chosen, counts, out):
+    slots = plan.slots
+    lane = lax.broadcasted_iota(jnp.int32, (SUB, slots), 1)
+    size = jnp.int32(0)
+    for c in chosen:
+        edge = lax.rem(size, slots)
+        block = lax.div(size, slots)
+        moved = pltpu.roll(fields[pl.ds(c, SUB, stride=cells), :], edge, 1)
+        out[block] = jnp.where(lane < edge, out[block], moved)
+        out[block + 1] = jnp.where(lane < edge, moved, 0.0)
+        size += counts[c]
+    return lax.div(size + (slots - 1), slots)
+
+
+def counts_of(fields, cells, chosen):
+    return {c: jnp.sum(jnp.where(fields[pl.ds(3 * cells + c, 1), :] > 0.0, 1.0, 0.0)).astype(jnp.int32) for c in chosen}
+
+
+def force_pairs(packed, blocks, limit, numbers, first, last, columns, press, sums, add):
+    def with_blocks(used):
+        def cell(o, carry):
+            def step(i, inner):
+                base = pl.multiple_of(i * ROWS, ROWS)
+                at = [pl.ds(base + r, SUB) for r in range(0, ROWS, SUB)]
+                own = [[*(columns[f, o, a, :] for f in range(3)), press[o, a, :]] for a in at]
+                total = [[sums[k, o, a, :] for k in range(4)] if add else [None] * 4 for a in at]
+                plus = lambda old, new: new if old is None else old + new
+                for b in range(used):
+                    x, y, z, m, c, *v = (packed[b, pl.ds(f, SUB, stride=0), :] for f in range(8))
+                    for r in range(len(at)):
+                        d = [own[r][0] - x, own[r][1] - y, own[r][2] - z]
+                        q = jnp.maximum(1.0 - (d[0] * d[0] + d[1] * d[1] + d[2] * d[2]), 0.0)
+                        q2 = q * q
+                        p = (m * own[r][3] + c) * q2
+                        w = c * (q2 * q)
+                        total[r][3] = plus(total[r][3], w)
+                        for f in range(3):
+                            total[r][f] = plus(total[r][f], p * d[f] + w * v[f])
+                for r, a in enumerate(at):
+                    for k in range(4):
+                        sums[k, o, a, :] = total[r][k]
+                return inner
+
+            lax.fori_loop(0, lax.div(numbers[o] + (ROWS - 1), ROWS), step, 0)
+            return carry
+
+        if last - first == 1:
+            cell(first, 0)
+        else:
+            lax.fori_loop(first, last, cell, 0)
+
+    for used in range(1, limit + 1):
+        pl.when(blocks == used)(functools.partial(with_blocks, used))
+
+
+def repeat(rows, out, slots):
+    count = rows.shape[0]
+    table = jnp.concatenate([rows, jnp.zeros((slots - count, slots), F32)], axis=0).T
+    for e in range(count):
+        out[e] = jnp.broadcast_to(table[:, e : e + 1], (slots, slots))
+
+
+def repeat_places_kernel(plan, state, out, placed):
+    place_cells(plan, Places(plan), state, placed, *(own_range(plan, k) for k in range(3)))
+    for f in range(3):
+        repeat(placed[pl.ds(f * plan.owns, plan.owns), :], out.at[f], plan.slots)
+
+
+def repeat_press_kernel(plan, flow, density, out, ordered):
+    places = Places(plan)
+    for o, cell in enumerate(plan.own_cells):
+        ordered[pl.ds(places.source(plan, cell), 1), :] = density[pl.ds(o, 1), :]
+    repeat(flow[pl.ds(3 * plan.owns, plan.owns), :], out, plan.slots)
+
+
+def note_numbers(plan, state, numbers):
+    for o, number in enumerate(numbers_of(state, plan)):
+        numbers[o] = number
+
+
+def force_own_kernel(plan, cells, flow, columns, press, sums, fields, placed, packed, numbers):
+    owns = plan.owns
+    note_numbers(plan, cells, numbers)
     place_cells(plan, Places(plan), cells, placed, *(own_range(plan, k) for k in range(3)))
-    rows = [placed[pl.ds(0, 3 * owns), :], flow[pl.ds(3 * owns, owns), :], jnp.zeros((slots - 4 * owns, slots), F32)]
-    table = jnp.concatenate(rows, axis=0).T
-    for f in range(4):
-        for o in range(owns):
-            e = f * owns + o
-            columns[f, o] = jnp.broadcast_to(table[:, e : e + 1], (slots, slots))
-    force_rows(extra, placed, flow, owns, 0)
-    for o, cell in enumerate(plan.own_cells):
-        near = [
-            lines_from(placed, flow, extra, owns, c, c)
-            for c, other in enumerate(plan.own_cells)
-            if max(abs(p - q) for p, q in zip(cell, other)) <= 1
-        ]
-        force_pairs(numbers[o], near, columns, o, None, sums)
-
-
-def force_block_kernel(plan, state, cells, flow, columns, start, sums, extra):
-    numbers = numbers_of(state, plan)
-    force_rows(extra, cells, flow, plan.cells, 0)
-    own = [plan.cell_index(*cell) for cell in plan.own_cells]
-    for o, (x, y, z) in enumerate(plan.own_cells):
-        near = [
-            lines_from(cells, flow, extra, plan.cells, c, c) for c in plan.near_cells(x, y, z) if c not in own
-        ]
-        force_pairs(numbers[o], near, columns, o, start, sums)
-
-
-def force_side_kernel(plan, state, flow, za, zb, fza, fzb, columns, start, accel, sums, extra):
-    slots, n, owns = plan.slots, plan.columns, plan.owns
-    numbers = numbers_of(state, plan)
+    gather_fields(fields, placed, flow, owns)
+    chosen = list(range(owns))
+    used = pack(plan, fields, owns, chosen, [numbers[o] for o in chosen], packed)
+    force_pairs(packed, used, owns, numbers, 0, owns, columns, press, sums, False)
+
+
+def force_block_kernel(plan, state, cells, flow, columns, press, start, sums, fields, packed, numbers):
+    note_numbers(plan, state, numbers)
+    gather_fields(fields, cells, flow, plan.cells)
+    mine = [plan.column_index(x, y) for x, y in plan.own_columns]
+    near = [
+        [k * plan.lz + z for k in plan.near_columns(x, y) if k not in mine for z in range(plan.lz)]
+        for x, y in plan.own_columns
+    ]
+    counts = counts_of(fields, plan.cells, sorted(set(sum(near, []))))
+    used = [pack(plan, fields, plan.cells, chosen, counts, packed.at[p]) for p, chosen in enumerate(near)]
+    for p, chosen in enumerate(near):
+        first = p * plan.lz
+        force_pairs(packed.at[p], used[p], len(chosen), numbers, first, first + plan.lz, columns, press, sums, True)
+
+
+def force_side(plan, side, state, near, flow, columns, press, sums, fields, packed, numbers):
+    n = plan.columns
+    note_numbers(plan, state, numbers)
+    gather_fields(fields, near, flow, n)
+    counts = counts_of(fields, n, range(n))
+    lists = [(o, plan.near_columns(*cell[:2])) for o, cell in plan.beside(side)]
+    used = [pack(plan, fields, n, chosen, counts, packed.at[p]) for p, (_, chosen) in enumerate(lists)]
+    for p, (o, chosen) in enumerate(lists):
+        force_pairs(packed.at[p], used[p], len(chosen), numbers, o, o + 1, columns, press, sums, True)
+
+
+def totals(plan, chosen, table):
+    lane = lax.broadcasted_iota(jnp.int32, table.shape, 1)
+    for o, sums in chosen:
+        for k in range(4):
+            table = jnp.where(lane == k * plan.owns + o, jnp.sum(sums[k, o], axis=1, keepdims=True), table)
+    return table
+
+
+def force_above_kernel(plan, state, near, flow, columns, press, start, sums, table, *scratch):
+    force_side(plan, 0, state, near, flow, columns, press, sums, *scratch)
+    mine = [] if plan.lz == 1 else [(o, sums) for o, _ in plan.beside(0)]
+    table[...] = totals(plan, mine, jnp.zeros(table.shape, F32))
+
+
+def force_below_kernel(plan, state, own, near, flow, columns, press, start, above, sums, accel, *scratch):
+    owns = plan.owns
+    force_side(plan, 1, state, near, flow, columns, press, sums, *scratch)
+    known = [] if plan.lz == 1 else [o for o, _ in plan.beside(0)]
+    mine = [(o, sums) for o in range(owns) if o not in known]
+    whole = totals(plan, mine, above[...]).T
     places = Places(plan)
-    for side, (ref, fref) in enumerate(((za, fza), (zb, fzb))):
-        force_rows(extra, ref, fref, n, side * n)
-    for o, (x, y, z) in enumerate(plan.own_cells):
-        near = []
-        for e in plan.near_sides(x, y, z):
-            side, k = divmod(e, n)
-            near.append(lines_from((za, zb)[side], (fza, fzb)[side], extra, n, k, e))
-        force_pairs(numbers[o], near, columns, o, start, sums)
-    lane = lax.broadcasted_iota(jnp.int32, (slots, slots), 1)
-    table = jnp.zeros((slots, slots), F32)
-    for e in range(4 * owns):
-        table = jnp.where(lane == e, jnp.sum(sums[e // owns, e % owns], axis=1, keepdims=True), table)
-    whole = table.T
-    for o, cell in enumerate(plan.own_cells):
-        at = places.source(plan, cell)
-        full = state[pl.ds(3 * owns + o, 1), :] > 0.0
-        for f in range(3):
-            v = flow[pl.ds(f * owns + o, 1), :]
-            value = 6.0 * (whole[f * owns + o : f * owns + o + 1] - v * whole[3 * owns + o : 3 * owns + o + 1])
-            accel[pl.ds(f * owns + at, 1), :] = jnp.where(full, value, 0.0)
+    full = state[pl.ds(3 * owns, owns), :] > 0.0
+    for f in range(3):
+        v = own[pl.ds(f * owns, owns), :]
+        value = 6.0 * (whole[f * owns : (f + 1) * owns] - v * whole[3 * owns : 4 * owns])
+        value = jnp.where(full, value, 0.0)
+        for o, cell in enumerate(plan.own_cells):
+            accel[pl.ds(f * owns + places.source(plan, cell), 1), :] = value[o : o + 1, :]
 
 
 def call(kernel, args, outs, scratch, cost, aliases=None):
@@ -403,14 +482,21 @@
             sides.append(flat(swap(message, sizes, "gz", kind) if present else jnp.zeros_like(message)))
         return flat(block), sides
 
-    number = jnp.broadcast_to(counts.astype(F32)[..., None], mass.shape)
-    fields = flat(jnp.concatenate([offsets, velocity, mass[None], number[None]], axis=0))
+    fields = flat(jnp.concatenate([offsets, velocity, mass[None]], axis=0))
     state, speed = call(
         functools.partial(prepare_kernel, plan),
-        [fields],
-        [((4 * owns, slots), F32), ((4 * owns, slots), F32)],
+        [fields, counts],
+        [((4 * owns, slots), F32), ((3 * owns, slots), F32)],
         [],
         1 << 20,
+    )
+    wide = (owns, slots, slots)
+    (places,) = call(
+        functools.partial(repeat_places_kernel, plan),
+        [state],
+        [((3,) + wide, F32)],
+        [pltpu.VMEM((4 * owns, slots), F32)],
+        1 << 26,
     )
     raw, (raw_a, raw_b) = gather(state)
     cells, right, sums = call(
@@ -429,36 +515,67 @@
         1 << 27,
     )
     side = ((4 * columns, slots), F32)
-    za, zb, flow_state, density = call(
-        functools.partial(density_side_kernel, plan),
-        [raw_a, raw_b, state, speed, right, sums],
-        [side, side, ((4 * owns, slots), F32), ((owns, slots), F32)],
-        [pltpu.VMEM((2 * columns * DEPTH, slots), F32), pltpu.VMEM((2 * columns * slots, DEPTH), BF16)],
-        1 << 26,
+    side_scratch = [pltpu.VMEM((columns * DEPTH, slots), F32), pltpu.VMEM((columns * slots, DEPTH), BF16)]
+    za, sums = call(
+        functools.partial(density_above_kernel, plan),
+        [raw_a, right, sums],
+        [side, ((pairs, SUB, lz * slots), F32)],
+        side_scratch,
+        1 << 25,
+    )
+    zb, flow_state, density = call(
+        functools.partial(density_below_kernel, plan),
+        [raw_b, state, speed, right, sums],
+        [side, ((4 * owns, slots), F32), ((owns, slots), F32)],
+        side_scratch,
+        1 << 25,
     )
     flow, (fza, fzb) = gather(flow_state)
-    wide = (4, owns, slots, slots)
-    repeated, partial = call(
+    press, density = call(
+        functools.partial(repeat_press_kernel, plan),
+        [flow_state, density],
+        [(wide, F32), ((owns, slots), F32)],
+        [],
+        1 << 25,
+    )
+    four = ((4,) + wide, F32)
+    numbers = pltpu.SMEM((owns,), jnp.int32)
+
+    def scratch_of(cells, lists, most):
+        return [pltpu.VMEM((8 * cells, slots), F32), pltpu.VMEM((*lists, most + 2, SUB, slots), F32), numbers]
+
+    most = max(len(plan.near_columns(*cell[:2])) for cell in plan.own_cells)
+    fields, packed, _ = scratch_of(owns, (), owns)
+    (partial,) = call(
         functools.partial(force_own_kernel, plan),
-        [state, flow_state],
-        [(wide, F32), (wide, F32)],
-        [pltpu.VMEM((2, owns, slots), F32), pltpu.VMEM((4 * owns, slots), F32)],
+        [state, flow_state, places, press],
+        [four],
+        [fields, pltpu.VMEM((4 * owns, slots), F32), packed, numbers],
         1 << 27,
     )
     (partial,) = call(
         functools.partial(force_block_kernel, plan),
-        [state, cells, flow, repeated, partial],
-        [(wide, F32)],
-        [pltpu.VMEM((2, total, slots), F32)],
+        [state, cells, flow, places, press, partial],
+        [four],
+        scratch_of(total, (pairs,), most * lz),
         1 << 27,
-        {4: 0},
-    )
-    (force,) = call(
-        functools.partial(force_side_kernel, plan),
-        [state, flow_state, za, zb, fza, fzb, repeated, partial],
-        [((3 * owns, slots), F32)],
-        [pltpu.VMEM(wide, F32), pltpu.VMEM((2, 2 * columns, slots), F32)],
-        1 << 27,
+        {5: 0},
+    )
+    partial, table = call(
+        functools.partial(force_above_kernel, plan),
+        [state, za, fza, places, press, partial],
+        [four, ((slots, slots), F32)],
+        scratch_of(columns, (pairs,), most),
+        1 << 26,
+        {5: 0},
+    )
+    _, force = call(
+        functools.partial(force_below_kernel, plan),
+        [state, flow_state, zb, fzb, places, press, partial, table],
+        [four, ((3 * owns, slots), F32)],
+        scratch_of(columns, (pairs,), most),
+        1 << 26,
+        {6: 0},
     )
     return force.reshape(offsets.shape), density.reshape(mass.shape)
 
@@ -476,6 +593,9 @@
         P("gx", "gy", "gz"),
     )
     out_specs = (P(None, "gx", "gy", "gz", None), P("gx", "gy", "gz", None))
-    return jax.shard_map(
+    step = jax.shard_map(
         functools.partial(layer, sizes), mesh=mesh, in_specs=in_specs, out_specs=out_specs, check_vma=False
     )
+    if min(sizes[a] for a in AXES) < 2:
+        return step
+    return step

time: 34.9 us -> 32.5 us (0.931)
  the two profiles are of different devices: /device:TPU:0 before, /device:TPU:12 now
where the time goes in v1:
time: 32.5 us; the launch traced here: 32 us
  Pallas kernels  12.2 us (38%)
  waiting for transfers between devices  9.12 us (28%)
  starting transfers between devices  8.08 us (25%)
  between operations  0.85 us (3%)
  local copies, waits for them, and re-layouts  0.84 us (3%)
  other arithmetic  0.83 us (3%)
    pallas_call x10, Pallas kernels, call(): pl.pallas_call(kernel, out_shape=[jax.ShapeDtypeStruct(shape, dtype) for...  12.2 us
    ppermute x10, waiting for transfers between devices, swap(): return lax.ppermute(message, names, pairs)  9.12 us
    ppermute x10, starting transfers between devices, swap(): return lax.ppermute(message, names, pairs)  8.08 us
    concatenate x1, other arithmetic, local(): fields = flat(jnp.concatenate([offsets, velocity, mass[None]], axis=0))  0.76 us
    unnamed x6, local copies, waits for them, and re-layouts  0.71 us
  transfers between devices with their start and end apart: 10, of which 6 were waited for; matrix products, arithmetic and copies ran while one was open for 0% of the time, Pallas kernels for 28%

profile of v1, /device:TPU:12, one launch (start us, length us, event | category | flops | bytes accessed | tf_op | source)
XLA Modules:
  0.0 32.0 jit_solution(12102064982864218956)
XLA Ops:
  0.6 0.8 %pad_maximum_fusion.2 = f32[7,2,2,2,128]{4,3,2,1,0:T(2,128)S(1)} fusion(f32[1,2,2,2,128]{4,3,2,1,0:T(2,128)} %bitcast.23, f32[3,2,2,2,128]{4,3,2,1,0:T(2,128)} %param.5, f32[3,2,2,2,128]{4,3,2,1,0:T(2,128)} %param.4), kind=kLoop, calls=%fused_computation.2 | loop fusion | flops 14336 | bytes 57344 | tf_op jit(solution)/shard_map/concatenate | solution.py:485
  1.4 0.7 %copy-done = s32[2,2,2]{2,1,0:T(2,128)S(1)} copy-done((s32[2,2,2]{2,1,0:T(2,128)S(1)}, s32[2,2,2]{2,1,0:T(2,128)}, u32[]{:S(2)}) %copy-start) | copy-done | bytes 56
  2.1 0.2 shard_map.59
  2.4 1.1 %collective-permute-done = f32[4,1,2,2,128]{4,2,1,0,3:T(2,128)S(1)} collective-permute-done((f32[4,1,2,2,128]{4,2,1,0,3:T(2,128)S(1)}, f32[4,1,2,2,128]{4,2,1,0,3:T(2,128)S(1)}, u32[]{:S(2)}, u32[]{:S(2)}) %collective-permute-start) | collective-permute-done | bytes 8224 | tf_op jit(solution)/shard_map/ppermute | solution.py:42
  3.5 1.6 %collective-permute-start.1 = (f32[4,3,1,2,128]{4,2,1,0,3:T(1,128)S(1)}, f32[4,3,1,2,128]{4,2,1,0,3:T(1,128)S(1)}, u32[]{:S(2)}, u32[]{:S(2)}) collective-permute-start(f32[4,3,1,2,128]{4,2,1,0,3:T(1,128)S(1)} %get-tuple-element.38), channel_id=1, source_target_pairs={{0,4},{4,0},{8,12},{12,8},{1,5},{5,1},{9,13},{13,9},{2,6},{6,2},{1... | collective-permute-start | bytes 36872 | tf_op jit(solution)/shard_map/ppermute | solution.py:42
  5.1 0.5 %collective-permute-start.2 = (f32[4,3,1,2,128]{4,2,1,0,3:T(1,128)S(1)}, f32[4,3,1,2,128]{4,2,1,0,3:T(1,128)S(1)}, u32[]{:S(2)}, u32[]{:S(2)}) collective-permute-start(f32[4,3,1,2,128]{4,2,1,0,3:T(1,128)S(1)} %get-tuple-element.39), channel_id=1, source_target_pairs={{0,16},{4,8},{8,4},{12,28},{16,0},{20,24},{24,20},{28,12},{1,17},{... | collective-permute-start | bytes 36872 | tf_op jit(solution)/shard_map/ppermute | solution.py:42
  5.6 1.7 %collective-permute-done.1 = f32[4,3,1,2,128]{4,2,1,0,3:T(1,128)S(1)} collective-permute-done((f32[4,3,1,2,128]{4,2,1,0,3:T(1,128)S(1)}, f32[4,3,1,2,128]{4,2,1,0,3:T(1,128)S(1)}, u32[]{:S(2)}, u32[]{:S(2)}) %collective-permute-start.1) | collective-permute-done | bytes 12320 | tf_op jit(solution)/shard_map/ppermute | solution.py:42
  7.3 2.4 %collective-permute-done.2 = f32[4,3,1,2,128]{4,2,1,0,3:T(1,128)S(1)} collective-permute-done((f32[4,3,1,2,128]{4,2,1,0,3:T(1,128)S(1)}, f32[4,3,1,2,128]{4,2,1,0,3:T(1,128)S(1)}, u32[]{:S(2)}, u32[]{:S(2)}) %collective-permute-start.2) | collective-permute-done | bytes 12320 | tf_op jit(solution)/shard_map/ppermute | solution.py:42
  9.7 0.5 %collective-permute-start.4 = (f32[4,3,4,1,128]{4,2,1,0,3:T(4,128)S(1)}, f32[4,3,4,1,128]{4,2,1,0,3:T(4,128)S(1)}, u32[]{:S(2)}, u32[]{:S(2)}) collective-permute-start(f32[4,3,4,1,128]{4,2,1,0,3:T(4,128)S(1)} %get-tuple-element.34), channel_id=1, source_target_pairs={{0,1},{1,0},{2,3},{3,2},{4,5},{5,4},{6,7},{7,6},{8,9},{9,8},{10,11... | collective-permute-start | bytes 73736 | tf_op jit(solution)/shard_map/ppermute | solution.py:42
  10.3 2.7 %collective-permute-start.3 = (f32[4,3,4,1,128]{4,2,1,0,3:T(4,128)S(1)}, f32[4,3,4,1,128]{4,2,1,0,3:T(4,128)S(1)}, u32[]{:S(2)}, u32[]{:S(2)}) collective-permute-start(f32[4,3,4,1,128]{4,2,1,0,3:T(4,128)S(1)} %get-tuple-element.35), channel_id=1, source_target_pairs={{0,16},{1,2},{2,1},{3,19},{16,0},{17,18},{18,17},{19,3},{4,20},{5,... | collective-permute-start | bytes 73736 | tf_op jit(solution)/shard_map/ppermute | solution.py:42
  13.0 1.8 %shard_map.60 = (f32[96,128]{1,0:T(8,128)S(1)}, bf16[4,32,256]{2,1,0:T(8,128)(2,1)S(1)}, f32[4,8,256]{2,1,0:T(8,128)S(1)}) custom-call(f32[96,128]{1,0:T(8,128)S(1)} %bitcast.18), custom_call_target="tpu_custom_call" | custom-call | flops 134217728 | bytes 1048576 | tf_op jit(solution)/shard_map/pallas_call | solution.py:455
  14.8 0.6 %shard_map.61 = (f32[48,128]{1,0:T(8,128)S(1)}, f32[4,8,256]{2,1,0:T(8,128)S(1)}) custom-call(f32[48,128]{1,0:T(8,128)S(1)} %bitcast.22, bf16[4,32,256]{2,1,0:T(8,128)(2,1)S(1)} %get-tuple-element.19.right, f32[4,8,256]{2,1,0:T(8,128)S(1)} %get-tuple-element.20.sums), custom_call_target="tpu_custom_call" | custom-call | flops 33554432 | bytes 1048576 | tf_op jit(solution)/shard_map/pallas_call | solution.py:455
  15.4 0.7 %shard_map.62 = (f32[48,128]{1,0:T(8,128)S(1)}, f32[32,128]{1,0:T(8,128)S(1)}, f32[8,128]{1,0:T(8,128)S(1)}) custom-call(f32[48,128]{1,0:T(8,128)S(1)} %bitcast.21, f32[32,128]{1,0:T(8,128)S(1)} %get-tuple-element.17.state.cells, f32[24,128]{1,0:T(8,128)S(1)} %get-tuple-element.18.speed, bf16[4,32,256]{2,1,0:T(8,128)(2,1)S(1)} %get-tuple-element.19.right, ...), custom_call_target="tpu_custom_call" | custom-call | flops 33554432 | bytes 1048576 | tf_op jit(solution)/shard_map/pallas_call | solution.py:455
  16.2 1.1 %collective-permute-done.5 = f32[4,1,2,2,128]{4,2,1,0,3:T(2,128)S(1)} collective-permute-done((f32[4,1,2,2,128]{4,2,1,0,3:T(2,128)S(1)}, f32[4,1,2,2,128]{4,2,1,0,3:T(2,128)S(1)}, u32[]{:S(2)}, u32[]{:S(2)}) %collective-permute-start.5) | collective-permute-done | bytes 8224 | tf_op jit(solution)/shard_map/ppermute | solution.py:42
  17.5 0.5 %collective-permute-start.7 = (f32[4,3,1,2,128]{4,2,1,0,3:T(1,128)S(1)}, f32[4,3,1,2,128]{4,2,1,0,3:T(1,128)S(1)}, u32[]{:S(2)}, u32[]{:S(2)}) collective-permute-start(f32[4,3,1,2,128]{4,2,1,0,3:T(1,128)S(1)} %get-tuple-element.37), channel_id=1, source_target_pairs={{0,16},{4,8},{8,4},{12,28},{16,0},{20,24},{24,20},{28,12},{1,17},{... | collective-permute-start | bytes 36872 | tf_op jit(solution)/shard_map/ppermute | solution.py:42
  18.0 0.6 %shard_map.63.columns = f32[3,8,128,128]{3,2,1,0:T(8,128)S(1)} custom-call(f32[32,128]{1,0:T(8,128)S(1)} %get-tuple-element.17.state.cells), custom_call_target="tpu_custom_call" | custom-call | flops 67108864 | bytes 1048576 | tf_op jit(solution)/shard_map/pallas_call | solution.py:455
  18.6 0.8 %shard_map.64 = (f32[8,128,128]{2,1,0:T(8,128)S(1)}, f32[8,128]{1,0:T(8,128)}) custom-call(f32[32,128]{1,0:T(8,128)S(1)} %get-tuple-element.22.flow.own, f32[8,128]{1,0:T(8,128)S(1)} %get-tuple-element.24.density), custom_call_target="tpu_custom_call" | custom-call | flops 33554432 | bytes 1048576 | tf_op jit(solution)/shard_map/pallas_call | solution.py:455
  19.4 1.7 %collective-permute-done.6 = f32[4,3,1,2,128]{4,2,1,0,3:T(1,128)S(1)} collective-permute-done((f32[4,3,1,2,128]{4,2,1,0,3:T(1,128)S(1)}, f32[4,3,1,2,128]{4,2,1,0,3:T(1,128)S(1)}, u32[]{:S(2)}, u32[]{:S(2)}) %collective-permute-start.6) | collective-permute-done | bytes 12320 | tf_op jit(solution)/shard_map/ppermute | solution.py:42
  21.1 1.0 %collective-permute-done.7 = f32[4,3,1,2,128]{4,2,1,0,3:T(1,128)S(1)} collective-permute-done((f32[4,3,1,2,128]{4,2,1,0,3:T(1,128)S(1)}, f32[4,3,1,2,128]{4,2,1,0,3:T(1,128)S(1)}, u32[]{:S(2)}, u32[]{:S(2)}) %collective-permute-start.7) | collective-permute-done | bytes 12320 | tf_op jit(solution)/shard_map/ppermute | solution.py:42
  22.2 2.0 %collective-permute-start.8 = (f32[4,3,4,1,128]{4,2,1,0,3:T(4,128)S(1)}, f32[4,3,4,1,128]{4,2,1,0,3:T(4,128)S(1)}, u32[]{:S(2)}, u32[]{:S(2)}) collective-permute-start(f32[4,3,4,1,128]{4,2,1,0,3:T(4,128)S(1)} %get-tuple-element.33), channel_id=1, source_target_pairs={{0,16},{1,2},{2,1},{3,19},{16,0},{17,18},{18,17},{19,3},{4,20},{5,... | collective-permute-start | bytes 73736 | tf_op jit(solution)/shard_map/ppermute | solution.py:42
  24.3 1.6 %shard_map.65.start = f32[4,8,128,128]{3,2,1,0:T(8,128)S(1)} custom-call(f32[32,128]{1,0:T(8,128)S(1)} %get-tuple-element.17.state.cells, f32[32,128]{1,0:T(8,128)S(1)} %get-tuple-element.22.flow.own, f32[3,8,128,128]{3,2,1,0:T(8,128)S(1)} %shard_map.63.columns, f32[8,128,128]{2,1,0:T(8,128)S(1)} %get-tuple-element.25.press), custom_call_target="tpu_custom_call" | custom-call | flops 134217728 | bytes 1048576 | tf_op jit(solution)/shard_map/pallas_call | solution.py:455
  25.9 2.0 %shard_map.66.start = f32[4,8,128,128]{3,2,1,0:T(8,128)S(1)} custom-call(f32[32,128]{1,0:T(8,128)S(1)} %get-tuple-element.17.state.cells, f32[96,128]{1,0:T(8,128)S(1)} %get-tuple-element.27.cells, f32[96,128]{1,0:T(8,128)S(1)} %bitcast.16, f32[3,8,128,128]{3,2,1,0:T(8,128)S(1)} %shard_map.63.columns, ...), custom_call_target="tpu_custom_call", output_to_operand_aliasing={{}: (5, {})} | custom-call | flops 134217728 | bytes 1048576 | tf_op jit(solution)/shard_map/pallas_call | solution.py:455
  27.9 1.7 %shard_map.67 = (f32[4,8,128,128]{3,2,1,0:T(8,128)S(1)}, f32[128,128]{1,0:T(8,128)S(1)}) custom-call(f32[32,128]{1,0:T(8,128)S(1)} %get-tuple-element.17.state.cells, f32[48,128]{1,0:T(8,128)S(1)} %get-tuple-element.26.near, f32[48,128]{1,0:T(8,128)S(1)} %bitcast.20, f32[3,8,128,128]{3,2,1,0:T(8,128)S(1)} %shard_map.63.columns, ...), custom_call_target="tpu_custom_call", output_to_operand_aliasing={{0}: (5, {})} | custom-call | flops 67108864 | bytes 1048576 | tf_op jit(solution)/shard_map/pallas_call | solution.py:455
  29.6 2.4 %shard_map.68 = (f32[4,8,128,128]{3,2,1,0:T(8,128)S(1)}, f32[24,128]{1,0:T(8,128)}) custom-call(f32[32,128]{1,0:T(8,128)S(1)} %get-tuple-element.17.state.cells, f32[32,128]{1,0:T(8,128)S(1)} %get-tuple-element.22.flow.own, f32[48,128]{1,0:T(8,128)S(1)} %get-tuple-element.23.near, f32[48,128]{1,0:T(8,128)S(1)} %bitcast.19, ...), custom_call_target="tpu_custom_call", output_to_operand_aliasing={{0}: (6, {})} | custom-call | flops 67108864 | bytes 1048576 | tf_op jit(solution)/shard_map/pallas_call | solution.py:455
  (25 shorter events, 0.5 us)
Async XLA Ops:
  1.4 0.7 %copy-start = (s32[2,2,2]{2,1,0:T(2,128)S(1)}, s32[2,2,2]{2,1,0:T(2,128)}, u32[]{:S(2)}) copy-start(s32[2,2,2]{2,1,0:T(2,128)} %counts.1) | copy-start | bytes 100
  2.3 1.2 %collective-permute-start = (f32[4,1,2,2,128]{4,2,1,0,3:T(2,128)S(1)}, f32[4,1,2,2,128]{4,2,1,0,3:T(2,128)S(1)}, u32[]{:S(2)}, u32[]{:S(2)}) collective-permute-start(f32[4,1,2,2,128]{4,2,1,0,3:T(2,128)S(1)} %copy.17), channel_id=1, source_target_pairs={{0,16},{16,0},{1,17},{17,1},{2,18},{18,2},{3,19},{19,3},{4,20},{20... | collective-permute-start | bytes 24584 | tf_op jit(solution)/shard_map/ppermute | solution.py:42
  3.5 3.8 %collective-permute-start.1 = (f32[4,3,1,2,128]{4,2,1,0,3:T(1,128)S(1)}, f32[4,3,1,2,128]{4,2,1,0,3:T(1,128)S(1)}, u32[]{:S(2)}, u32[]{:S(2)}) collective-permute-start(f32[4,3,1,2,128]{4,2,1,0,3:T(1,128)S(1)} %get-tuple-element.38), channel_id=1, source_target_pairs={{0,4},{4,0},{8,12},{12,8},{1,5},{5,1},{9,13},{13,9},{2,6},{6,2},{1... | collective-permute-start | bytes 36872 | tf_op jit(solution)/shard_map/ppermute | solution.py:42
  5.1 4.6 %collective-permute-start.2 = (f32[4,3,1,2,128]{4,2,1,0,3:T(1,128)S(1)}, f32[4,3,1,2,128]{4,2,1,0,3:T(1,128)S(1)}, u32[]{:S(2)}, u32[]{:S(2)}) collective-permute-start(f32[4,3,1,2,128]{4,2,1,0,3:T(1,128)S(1)} %get-tuple-element.39), channel_id=1, source_target_pairs={{0,16},{4,8},{8,4},{12,28},{16,0},{20,24},{24,20},{28,12},{1,17},{... | collective-permute-start | bytes 36872 | tf_op jit(solution)/shard_map/ppermute | solution.py:42
  9.7 5.0 %collective-permute-start.4 = (f32[4,3,4,1,128]{4,2,1,0,3:T(4,128)S(1)}, f32[4,3,4,1,128]{4,2,1,0,3:T(4,128)S(1)}, u32[]{:S(2)}, u32[]{:S(2)}) collective-permute-start(f32[4,3,4,1,128]{4,2,1,0,3:T(4,128)S(1)} %get-tuple-element.34), channel_id=1, source_target_pairs={{0,1},{1,0},{2,3},{3,2},{4,5},{5,4},{6,7},{7,6},{8,9},{9,8},{10,11... | collective-permute-start | bytes 73736 | tf_op jit(solution)/shard_map/ppermute | solution.py:42
  10.3 5.2 %collective-permute-start.3 = (f32[4,3,4,1,128]{4,2,1,0,3:T(4,128)S(1)}, f32[4,3,4,1,128]{4,2,1,0,3:T(4,128)S(1)}, u32[]{:S(2)}, u32[]{:S(2)}) collective-permute-start(f32[4,3,4,1,128]{4,2,1,0,3:T(4,128)S(1)} %get-tuple-element.35), channel_id=1, source_target_pairs={{0,16},{1,2},{2,1},{3,19},{16,0},{17,18},{18,17},{19,3},{4,20},{5,... | collective-permute-start | bytes 73736 | tf_op jit(solution)/shard_map/ppermute | solution.py:42
  16.1 1.2 %collective-permute-start.5 = (f32[4,1,2,2,128]{4,2,1,0,3:T(2,128)S(1)}, f32[4,1,2,2,128]{4,2,1,0,3:T(2,128)S(1)}, u32[]{:S(2)}, u32[]{:S(2)}) collective-permute-start(f32[4,1,2,2,128]{4,2,1,0,3:T(2,128)S(1)} %copy.18), channel_id=1, source_target_pairs={{0,16},{16,0},{1,17},{17,1},{2,18},{18,2},{3,19},{19,3},{4,20},{20... | collective-permute-start | bytes 24584 | tf_op jit(solution)/shard_map/ppermute | solution.py:42
  17.4 3.8 %collective-permute-start.6 = (f32[4,3,1,2,128]{4,2,1,0,3:T(1,128)S(1)}, f32[4,3,1,2,128]{4,2,1,0,3:T(1,128)S(1)}, u32[]{:S(2)}, u32[]{:S(2)}) collective-permute-start(f32[4,3,1,2,128]{4,2,1,0,3:T(1,128)S(1)} %get-tuple-element.36), channel_id=1, source_target_pairs={{0,4},{4,0},{8,12},{12,8},{1,5},{5,1},{9,13},{13,9},{2,6},{6,2},{1... | collective-permute-start | bytes 36872 | tf_op jit(solution)/shard_map/ppermute | solution.py:42
  17.5 4.7 %collective-permute-start.7 = (f32[4,3,1,2,128]{4,2,1,0,3:T(1,128)S(1)}, f32[4,3,1,2,128]{4,2,1,0,3:T(1,128)S(1)}, u32[]{:S(2)}, u32[]{:S(2)}) collective-permute-start(f32[4,3,1,2,128]{4,2,1,0,3:T(1,128)S(1)} %get-tuple-element.37), channel_id=1, source_target_pairs={{0,16},{4,8},{8,4},{12,28},{16,0},{20,24},{24,20},{28,12},{1,17},{... | collective-permute-start | bytes 36872 | tf_op jit(solution)/shard_map/ppermute | solution.py:42
  22.2 5.7 %collective-permute-start.9 = (f32[4,3,4,1,128]{4,2,1,0,3:T(4,128)S(1)}, f32[4,3,4,1,128]{4,2,1,0,3:T(4,128)S(1)}, u32[]{:S(2)}, u32[]{:S(2)}) collective-permute-start(f32[4,3,4,1,128]{4,2,1,0,3:T(4,128)S(1)} %get-tuple-element.32), channel_id=1, source_target_pairs={{0,1},{1,0},{2,3},{3,2},{4,5},{5,4},{6,7},{7,6},{8,9},{9,8},{10,11... | collective-permute-start | bytes 73736 | tf_op jit(solution)/shard_map/ppermute | solution.py:42
  22.2 7.3 %collective-permute-start.8 = (f32[4,3,4,1,128]{4,2,1,0,3:T(4,128)S(1)}, f32[4,3,4,1,128]{4,2,1,0,3:T(4,128)S(1)}, u32[]{:S(2)}, u32[]{:S(2)}) collective-permute-start(f32[4,3,4,1,128]{4,2,1,0,3:T(4,128)S(1)} %get-tuple-element.33), channel_id=1, source_target_pairs={{0,16},{1,2},{2,1},{3,19},{16,0},{17,18},{18,17},{19,3},{4,20},{5,... | collective-permute-start | bytes 73736 | tf_op jit(solution)/shard_map/ppermute | solution.py:42

commit v2 on v1

--- a/solution.py
+++ b/solution.py
@@ -205,9 +205,17 @@
         left[pl.ds(c * slots, slots), :] = staged[pl.ds(c * DEPTH, DEPTH), :].T.astype(BF16)
 
 
-def prepare_kernel(plan, fields, counts, state, speed):
+def prepare_kernel(plan, *refs):
+    state, speed = refs[4], refs[5]
+    fetched, sems = refs[6:10], refs[10]
+    copies = [pltpu.make_async_copy(a, b, sems.at[i]) for i, (a, b) in enumerate(zip(refs[:4], fetched))]
+    for copy in copies:
+        copy.start()
     owns, slots = plan.owns, plan.slots
     places = Places(plan)
+    for copy in copies:
+        copy.wait()
+    counts, mass, offsets, velocity = fetched
     row = lax.broadcasted_iota(jnp.int32, plan.extents[1:], 0)
     column = lax.broadcasted_iota(jnp.int32, plan.extents[1:], 1)
     line = lax.broadcasted_iota(jnp.int32, (owns, slots), 0)
@@ -218,8 +226,8 @@
         number = jnp.sum(jnp.where((row == y) & (column == z), counts[x].astype(F32), 0.0))
         held = jnp.where(line == o, number, held)
         for f in range(3):
-            state[pl.ds(f * owns + o, 1), :] = fields[pl.ds(f * owns + at, 1), :]
-        state[pl.ds(3 * owns + o, 1), :] = fields[pl.ds(6 * owns + at, 1), :]
+            state[pl.ds(f * owns + o, 1), :] = offsets[pl.ds(f * owns + at, 1), :]
+        state[pl.ds(3 * owns + o, 1), :] = mass[pl.ds(at, 1), :]
     heavy = state[pl.ds(3 * owns, owns), :] * KERNEL_NORM
     root = jnp.exp(jnp.log(heavy) * (1.0 / 3.0))
     root = root * (2.0 / 3.0) + heavy / (3.0 * root * root)
@@ -228,7 +236,7 @@
     for o, cell in enumerate(plan.own_cells):
         at = places.source(plan, cell)
         for f in range(3):
-            speed[pl.ds(f * owns + o, 1), :] = fields[pl.ds((3 + f) * owns + at, 1), :] * (1.0 / 6.0)
+            speed[pl.ds(f * owns + o, 1), :] = velocity[pl.ds(f * owns + at, 1), :] * (1.0 / 6.0)
 
 
 def cubes(left, right):
@@ -450,12 +458,12 @@
             accel[pl.ds(f * owns + places.source(plan, cell), 1), :] = value[o : o + 1, :]
 
 
-def call(kernel, args, outs, scratch, cost, aliases=None):
+def call(kernel, args, outs, scratch, cost, aliases=None, place=pltpu.VMEM):
     vmem = pl.BlockSpec(memory_space=pltpu.VMEM)
     return pl.pallas_call(
         kernel,
         out_shape=[jax.ShapeDtypeStruct(shape, dtype) for shape, dtype in outs],
-        in_specs=[vmem] * len(args),
+        in_specs=[pl.BlockSpec(memory_space=place)] * len(args),
         out_specs=[vmem] * len(outs),
         scratch_shapes=scratch,
         input_output_aliases=aliases or {},
@@ -482,13 +490,20 @@
             sides.append(flat(swap(message, sizes, "gz", kind) if present else jnp.zeros_like(message)))
         return flat(block), sides
 
-    fields = flat(jnp.concatenate([offsets, velocity, mass[None]], axis=0))
+    stay = lambda x: pltpu.with_memory_space_constraint(x, pltpu.HBM)
     state, speed = call(
         functools.partial(prepare_kernel, plan),
-        [fields, counts],
+        [stay(counts), stay(flat(mass)), stay(flat(offsets)), stay(flat(velocity))],
         [((4 * owns, slots), F32), ((3 * owns, slots), F32)],
-        [],
+        [
+            pltpu.VMEM(tuple(extents), jnp.int32),
+            pltpu.VMEM((owns, slots), F32),
+            pltpu.VMEM((3 * owns, slots), F32),
+            pltpu.VMEM((3 * owns, slots), F32),
+            pltpu.SemaphoreType.DMA((4,)),
+        ],
         1 << 20,
+        place=pltpu.HBM,
     )
     wide = (owns, slots, slots)
     (places,) = call(

time: 32.5 us -> 31.7 us (0.975)
  Pallas kernels: 12.2 us -> 13 us
  other arithmetic: 0.83 us -> 0.08 us
  local copies, waits for them, and re-layouts: 0.84 us -> 0.16 us
    pallas_call x10, Pallas kernels: 12.2 us -> 13 us  [call(): pl.pallas_call(kernel, out_shape=[jax.ShapeDtypeStruct(shape, dtype) for...]
    concatenate x1 -> x0, other arithmetic: 0.76 us -> none  [local(): fields = flat(jnp.concatenate([offsets, velocity, mass[None]], axis=0))]
    unnamed x6 -> x4, local copies, waits for them, and re-layouts: 0.71 us -> 0.03 us
  transfers between devices with their start and end apart: 10 -> 10, of which waited for: 6 -> 6; matrix products, arithmetic and copies ran while one was open for 0% -> 0% of each run, Pallas kernels for 28% -> 29%
where the time goes in v2:
time: 31.7 us; the launch traced here: 31.3 us
  Pallas kernels  13 us (41%)
  waiting for transfers between devices  9.12 us (29%)
  starting transfers between devices  8.09 us (26%)
  between operations  0.84 us (3%)
    pallas_call x10, Pallas kernels, call(): pl.pallas_call(kernel, out_shape=[jax.ShapeDtypeStruct(shape, dtype) for...  13 us
    ppermute x10, waiting for transfers between devices, swap(): return lax.ppermute(message, names, pairs)  9.12 us
    ppermute x10, starting transfers between devices, swap(): return lax.ppermute(message, names, pairs)  8.09 us
  transfers between devices with their start and end apart: 10, of which 6 were waited for; matrix products, arithmetic and copies ran while one was open for 0% of the time, Pallas kernels for 29%

profile of v2, /device:TPU:12, one launch (start us, length us, event | category | flops | bytes accessed | tf_op | source)
XLA Modules:
  0.0 31.3 jit_solution(13135606990382312010)
XLA Ops:
  0.6 0.9 %shard_map.59 = (f32[32,128]{1,0:T(8,128)S(1)}, f32[24,128]{1,0:T(8,128)S(1)}) custom-call(s32[2,2,2]{2,1,0:T(2,128)} %refs_0_.1, f32[8,128]{1,0:T(8,128)} %bitcast.25, f32[24,128]{1,0:T(8,128)} %bitcast.23, f32[24,128]{1,0:T(8,128)} %bitcast.24), custom_call_target="tpu_custom_call" | custom-call | flops 1048576 | bytes 1048576 | tf_op jit(solution)/shard_map/pallas_call | solution.py:463
  1.7 1.1 %collective-permute-done = f32[4,1,2,2,128]{4,2,1,0,3:T(2,128)S(1)} collective-permute-done((f32[4,1,2,2,128]{4,2,1,0,3:T(2,128)S(1)}, f32[4,1,2,2,128]{4,2,1,0,3:T(2,128)S(1)}, u32[]{:S(2)}, u32[]{:S(2)}) %collective-permute-start) | collective-permute-done | bytes 8224 | tf_op jit(solution)/shard_map/ppermute | solution.py:42
  2.9 1.6 %collective-permute-start.1 = (f32[4,3,1,2,128]{4,2,1,0,3:T(1,128)S(1)}, f32[4,3,1,2,128]{4,2,1,0,3:T(1,128)S(1)}, u32[]{:S(2)}, u32[]{:S(2)}) collective-permute-start(f32[4,3,1,2,128]{4,2,1,0,3:T(1,128)S(1)} %get-tuple-element.38), channel_id=1, source_target_pairs={{0,4},{4,0},{8,12},{12,8},{1,5},{5,1},{9,13},{13,9},{2,6},{6,2},{1... | collective-permute-start | bytes 36872 | tf_op jit(solution)/shard_map/ppermute | solution.py:42
  4.4 0.5 %collective-permute-start.2 = (f32[4,3,1,2,128]{4,2,1,0,3:T(1,128)S(1)}, f32[4,3,1,2,128]{4,2,1,0,3:T(1,128)S(1)}, u32[]{:S(2)}, u32[]{:S(2)}) collective-permute-start(f32[4,3,1,2,128]{4,2,1,0,3:T(1,128)S(1)} %get-tuple-element.39), channel_id=1, source_target_pairs={{0,16},{4,8},{8,4},{12,28},{16,0},{20,24},{24,20},{28,12},{1,17},{... | collective-permute-start | bytes 36872 | tf_op jit(solution)/shard_map/ppermute | solution.py:42
  4.9 1.7 %collective-permute-done.1 = f32[4,3,1,2,128]{4,2,1,0,3:T(1,128)S(1)} collective-permute-done((f32[4,3,1,2,128]{4,2,1,0,3:T(1,128)S(1)}, f32[4,3,1,2,128]{4,2,1,0,3:T(1,128)S(1)}, u32[]{:S(2)}, u32[]{:S(2)}) %collective-permute-start.1) | collective-permute-done | bytes 12320 | tf_op jit(solution)/shard_map/ppermute | solution.py:42
  6.6 2.4 %collective-permute-done.2 = f32[4,3,1,2,128]{4,2,1,0,3:T(1,128)S(1)} collective-permute-done((f32[4,3,1,2,128]{4,2,1,0,3:T(1,128)S(1)}, f32[4,3,1,2,128]{4,2,1,0,3:T(1,128)S(1)}, u32[]{:S(2)}, u32[]{:S(2)}) %collective-permute-start.2) | collective-permute-done | bytes 12320 | tf_op jit(solution)/shard_map/ppermute | solution.py:42
  9.1 0.5 %collective-permute-start.4 = (f32[4,3,4,1,128]{4,2,1,0,3:T(4,128)S(1)}, f32[4,3,4,1,128]{4,2,1,0,3:T(4,128)S(1)}, u32[]{:S(2)}, u32[]{:S(2)}) collective-permute-start(f32[4,3,4,1,128]{4,2,1,0,3:T(4,128)S(1)} %get-tuple-element.34), channel_id=1, source_target_pairs={{0,1},{1,0},{2,3},{3,2},{4,5},{5,4},{6,7},{7,6},{8,9},{9,8},{10,11... | collective-permute-start | bytes 73736 | tf_op jit(solution)/shard_map/ppermute | solution.py:42
  9.6 2.7 %collective-permute-start.3 = (f32[4,3,4,1,128]{4,2,1,0,3:T(4,128)S(1)}, f32[4,3,4,1,128]{4,2,1,0,3:T(4,128)S(1)}, u32[]{:S(2)}, u32[]{:S(2)}) collective-permute-start(f32[4,3,4,1,128]{4,2,1,0,3:T(4,128)S(1)} %get-tuple-element.35), channel_id=1, source_target_pairs={{0,16},{1,2},{2,1},{3,19},{16,0},{17,18},{18,17},{19,3},{4,20},{5,... | collective-permute-start | bytes 73736 | tf_op jit(solution)/shard_map/ppermute | solution.py:42
  12.3 1.8 %shard_map.60 = (f32[96,128]{1,0:T(8,128)S(1)}, bf16[4,32,256]{2,1,0:T(8,128)(2,1)S(1)}, f32[4,8,256]{2,1,0:T(8,128)S(1)}) custom-call(f32[96,128]{1,0:T(8,128)S(1)} %bitcast.18), custom_call_target="tpu_custom_call" | custom-call | flops 134217728 | bytes 1048576 | tf_op jit(solution)/shard_map/pallas_call | solution.py:463
  14.1 0.6 %shard_map.61 = (f32[48,128]{1,0:T(8,128)S(1)}, f32[4,8,256]{2,1,0:T(8,128)S(1)}) custom-call(f32[48,128]{1,0:T(8,128)S(1)} %bitcast.22, bf16[4,32,256]{2,1,0:T(8,128)(2,1)S(1)} %get-tuple-element.19.right, f32[4,8,256]{2,1,0:T(8,128)S(1)} %get-tuple-element.20.sums), custom_call_target="tpu_custom_call" | custom-call | flops 33554432 | bytes 1048576 | tf_op jit(solution)/shard_map/pallas_call | solution.py:463
  14.8 0.7 %shard_map.62 = (f32[48,128]{1,0:T(8,128)S(1)}, f32[32,128]{1,0:T(8,128)S(1)}, f32[8,128]{1,0:T(8,128)S(1)}) custom-call(f32[48,128]{1,0:T(8,128)S(1)} %bitcast.21, f32[32,128]{1,0:T(8,128)S(1)} %get-tuple-element.17.state.cells, f32[24,128]{1,0:T(8,128)S(1)} %get-tuple-element.18.speed, bf16[4,32,256]{2,1,0:T(8,128)(2,1)S(1)} %get-tuple-element.19.right, ...), custom_call_target="tpu_custom_call" | custom-call | flops 33554432 | bytes 1048576 | tf_op jit(solution)/shard_map/pallas_call | solution.py:463
  15.4 0.1 collective-permute-start.5
  15.5 1.1 %collective-permute-done.5 = f32[4,1,2,2,128]{4,2,1,0,3:T(2,128)S(1)} collective-permute-done((f32[4,1,2,2,128]{4,2,1,0,3:T(2,128)S(1)}, f32[4,1,2,2,128]{4,2,1,0,3:T(2,128)S(1)}, u32[]{:S(2)}, u32[]{:S(2)}) %collective-permute-start.5) | collective-permute-done | bytes 8224 | tf_op jit(solution)/shard_map/ppermute | solution.py:42
  16.8 0.5 %collective-permute-start.7 = (f32[4,3,1,2,128]{4,2,1,0,3:T(1,128)S(1)}, f32[4,3,1,2,128]{4,2,1,0,3:T(1,128)S(1)}, u32[]{:S(2)}, u32[]{:S(2)}) collective-permute-start(f32[4,3,1,2,128]{4,2,1,0,3:T(1,128)S(1)} %get-tuple-element.37), channel_id=1, source_target_pairs={{0,16},{4,8},{8,4},{12,28},{16,0},{20,24},{24,20},{28,12},{1,17},{... | collective-permute-start | bytes 36872 | tf_op jit(solution)/shard_map/ppermute | solution.py:42
  17.3 0.6 %shard_map.63.columns = f32[3,8,128,128]{3,2,1,0:T(8,128)S(1)} custom-call(f32[32,128]{1,0:T(8,128)S(1)} %get-tuple-element.17.state.cells), custom_call_target="tpu_custom_call" | custom-call | flops 67108864 | bytes 1048576 | tf_op jit(solution)/shard_map/pallas_call | solution.py:463
  17.9 0.8 %shard_map.64 = (f32[8,128,128]{2,1,0:T(8,128)S(1)}, f32[8,128]{1,0:T(8,128)}) custom-call(f32[32,128]{1,0:T(8,128)S(1)} %get-tuple-element.22.flow.own, f32[8,128]{1,0:T(8,128)S(1)} %get-tuple-element.24.density), custom_call_target="tpu_custom_call" | custom-call | flops 33554432 | bytes 1048576 | tf_op jit(solution)/shard_map/pallas_call | solution.py:463
  18.7 1.7 %collective-permute-done.6 = f32[4,3,1,2,128]{4,2,1,0,3:T(1,128)S(1)} collective-permute-done((f32[4,3,1,2,128]{4,2,1,0,3:T(1,128)S(1)}, f32[4,3,1,2,128]{4,2,1,0,3:T(1,128)S(1)}, u32[]{:S(2)}, u32[]{:S(2)}) %collective-permute-start.6) | collective-permute-done | bytes 12320 | tf_op jit(solution)/shard_map/ppermute | solution.py:42
  20.5 1.0 %collective-permute-done.7 = f32[4,3,1,2,128]{4,2,1,0,3:T(1,128)S(1)} collective-permute-done((f32[4,3,1,2,128]{4,2,1,0,3:T(1,128)S(1)}, f32[4,3,1,2,128]{4,2,1,0,3:T(1,128)S(1)}, u32[]{:S(2)}, u32[]{:S(2)}) %collective-permute-start.7) | collective-permute-done | bytes 12320 | tf_op jit(solution)/shard_map/ppermute | solution.py:42
  21.5 0.1 collective-permute-start.9
  21.6 2.0 %collective-permute-start.8 = (f32[4,3,4,1,128]{4,2,1,0,3:T(4,128)S(1)}, f32[4,3,4,1,128]{4,2,1,0,3:T(4,128)S(1)}, u32[]{:S(2)}, u32[]{:S(2)}) collective-permute-start(f32[4,3,4,1,128]{4,2,1,0,3:T(4,128)S(1)} %get-tuple-element.33), channel_id=1, source_target_pairs={{0,16},{1,2},{2,1},{3,19},{16,0},{17,18},{18,17},{19,3},{4,20},{5,... | collective-permute-start | bytes 73736 | tf_op jit(solution)/shard_map/ppermute | solution.py:42
  23.6 1.6 %shard_map.65.start = f32[4,8,128,128]{3,2,1,0:T(8,128)S(1)} custom-call(f32[32,128]{1,0:T(8,128)S(1)} %get-tuple-element.17.state.cells, f32[32,128]{1,0:T(8,128)S(1)} %get-tuple-element.22.flow.own, f32[3,8,128,128]{3,2,1,0:T(8,128)S(1)} %shard_map.63.columns, f32[8,128,128]{2,1,0:T(8,128)S(1)} %get-tuple-element.25.press), custom_call_target="tpu_custom_call" | custom-call | flops 134217728 | bytes 1048576 | tf_op jit(solution)/shard_map/pallas_call | solution.py:463
  25.2 2.0 %shard_map.66.start = f32[4,8,128,128]{3,2,1,0:T(8,128)S(1)} custom-call(f32[32,128]{1,0:T(8,128)S(1)} %get-tuple-element.17.state.cells, f32[96,128]{1,0:T(8,128)S(1)} %get-tuple-element.27.cells, f32[96,128]{1,0:T(8,128)S(1)} %bitcast.17, f32[3,8,128,128]{3,2,1,0:T(8,128)S(1)} %shard_map.63.columns, ...), custom_call_target="tpu_custom_call", output_to_operand_aliasing={{}: (5, {})} | custom-call | flops 134217728 | bytes 1048576 | tf_op jit(solution)/shard_map/pallas_call | solution.py:463
  27.3 1.7 %shard_map.67 = (f32[4,8,128,128]{3,2,1,0:T(8,128)S(1)}, f32[128,128]{1,0:T(8,128)S(1)}) custom-call(f32[32,128]{1,0:T(8,128)S(1)} %get-tuple-element.17.state.cells, f32[48,128]{1,0:T(8,128)S(1)} %get-tuple-element.26.near, f32[48,128]{1,0:T(8,128)S(1)} %bitcast.20, f32[3,8,128,128]{3,2,1,0:T(8,128)S(1)} %shard_map.63.columns, ...), custom_call_target="tpu_custom_call", output_to_operand_aliasing={{0}: (5, {})} | custom-call | flops 67108864 | bytes 1048576 | tf_op jit(solution)/shard_map/pallas_call | solution.py:463
  28.9 2.4 %shard_map.68 = (f32[4,8,128,128]{3,2,1,0:T(8,128)S(1)}, f32[24,128]{1,0:T(8,128)}) custom-call(f32[32,128]{1,0:T(8,128)S(1)} %get-tuple-element.17.state.cells, f32[32,128]{1,0:T(8,128)S(1)} %get-tuple-element.22.flow.own, f32[48,128]{1,0:T(8,128)S(1)} %get-tuple-element.23.near, f32[48,128]{1,0:T(8,128)S(1)} %bitcast.19, ...), custom_call_target="tpu_custom_call", output_to_operand_aliasing={{0}: (6, {})} | custom-call | flops 67108864 | bytes 1048576 | tf_op jit(solution)/shard_map/pallas_call | solution.py:463
  (22 shorter events, 0.4 us)
Async XLA Ops:
  1.6 1.2 %collective-permute-start = (f32[4,1,2,2,128]{4,2,1,0,3:T(2,128)S(1)}, f32[4,1,2,2,128]{4,2,1,0,3:T(2,128)S(1)}, u32[]{:S(2)}, u32[]{:S(2)}) collective-permute-start(f32[4,1,2,2,128]{4,2,1,0,3:T(2,128)S(1)} %copy.17), channel_id=1, source_target_pairs={{0,16},{16,0},{1,17},{17,1},{2,18},{18,2},{3,19},{19,3},{4,20},{20... | collective-permute-start | bytes 24584 | tf_op jit(solution)/shard_map/ppermute | solution.py:42
  2.9 3.8 %collective-permute-start.1 = (f32[4,3,1,2,128]{4,2,1,0,3:T(1,128)S(1)}, f32[4,3,1,2,128]{4,2,1,0,3:T(1,128)S(1)}, u32[]{:S(2)}, u32[]{:S(2)}) collective-permute-start(f32[4,3,1,2,128]{4,2,1,0,3:T(1,128)S(1)} %get-tuple-element.38), channel_id=1, source_target_pairs={{0,4},{4,0},{8,12},{12,8},{1,5},{5,1},{9,13},{13,9},{2,6},{6,2},{1... | collective-permute-start | bytes 36872 | tf_op jit(solution)/shard_map/ppermute | solution.py:42
  4.4 4.6 %collective-permute-start.2 = (f32[4,3,1,2,128]{4,2,1,0,3:T(1,128)S(1)}, f32[4,3,1,2,128]{4,2,1,0,3:T(1,128)S(1)}, u32[]{:S(2)}, u32[]{:S(2)}) collective-permute-start(f32[4,3,1,2,128]{4,2,1,0,3:T(1,128)S(1)} %get-tuple-element.39), channel_id=1, source_target_pairs={{0,16},{4,8},{8,4},{12,28},{16,0},{20,24},{24,20},{28,12},{1,17},{... | collective-permute-start | bytes 36872 | tf_op jit(solution)/shard_map/ppermute | solution.py:42
  9.1 5.0 %collective-permute-start.4 = (f32[4,3,4,1,128]{4,2,1,0,3:T(4,128)S(1)}, f32[4,3,4,1,128]{4,2,1,0,3:T(4,128)S(1)}, u32[]{:S(2)}, u32[]{:S(2)}) collective-permute-start(f32[4,3,4,1,128]{4,2,1,0,3:T(4,128)S(1)} %get-tuple-element.34), channel_id=1, source_target_pairs={{0,1},{1,0},{2,3},{3,2},{4,5},{5,4},{6,7},{7,6},{8,9},{9,8},{10,11... | collective-permute-start | bytes 73736 | tf_op jit(solution)/shard_map/ppermute | solution.py:42
  9.6 5.2 %collective-permute-start.3 = (f32[4,3,4,1,128]{4,2,1,0,3:T(4,128)S(1)}, f32[4,3,4,1,128]{4,2,1,0,3:T(4,128)S(1)}, u32[]{:S(2)}, u32[]{:S(2)}) collective-permute-start(f32[4,3,4,1,128]{4,2,1,0,3:T(4,128)S(1)} %get-tuple-element.35), channel_id=1, source_target_pairs={{0,16},{1,2},{2,1},{3,19},{16,0},{17,18},{18,17},{19,3},{4,20},{5,... | collective-permute-start | bytes 73736 | tf_op jit(solution)/shard_map/ppermute | solution.py:42
  15.4 1.2 %collective-permute-start.5 = (f32[4,1,2,2,128]{4,2,1,0,3:T(2,128)S(1)}, f32[4,1,2,2,128]{4,2,1,0,3:T(2,128)S(1)}, u32[]{:S(2)}, u32[]{:S(2)}) collective-permute-start(f32[4,1,2,2,128]{4,2,1,0,3:T(2,128)S(1)} %copy.18), channel_id=1, source_target_pairs={{0,16},{16,0},{1,17},{17,1},{2,18},{18,2},{3,19},{19,3},{4,20},{20... | collective-permute-start | bytes 24584 | tf_op jit(solution)/shard_map/ppermute | solution.py:42
  16.7 3.8 %collective-permute-start.6 = (f32[4,3,1,2,128]{4,2,1,0,3:T(1,128)S(1)}, f32[4,3,1,2,128]{4,2,1,0,3:T(1,128)S(1)}, u32[]{:S(2)}, u32[]{:S(2)}) collective-permute-start(f32[4,3,1,2,128]{4,2,1,0,3:T(1,128)S(1)} %get-tuple-element.36), channel_id=1, source_target_pairs={{0,4},{4,0},{8,12},{12,8},{1,5},{5,1},{9,13},{13,9},{2,6},{6,2},{1... | collective-permute-start | bytes 36872 | tf_op jit(solution)/shard_map/ppermute | solution.py:42
  16.8 4.7 %collective-permute-start.7 = (f32[4,3,1,2,128]{4,2,1,0,3:T(1,128)S(1)}, f32[4,3,1,2,128]{4,2,1,0,3:T(1,128)S(1)}, u32[]{:S(2)}, u32[]{:S(2)}) collective-permute-start(f32[4,3,1,2,128]{4,2,1,0,3:T(1,128)S(1)} %get-tuple-element.37), channel_id=1, source_target_pairs={{0,16},{4,8},{8,4},{12,28},{16,0},{20,24},{24,20},{28,12},{1,17},{... | collective-permute-start | bytes 36872 | tf_op jit(solution)/shard_map/ppermute | solution.py:42
  21.5 5.7 %collective-permute-start.9 = (f32[4,3,4,1,128]{4,2,1,0,3:T(4,128)S(1)}, f32[4,3,4,1,128]{4,2,1,0,3:T(4,128)S(1)}, u32[]{:S(2)}, u32[]{:S(2)}) collective-permute-start(f32[4,3,4,1,128]{4,2,1,0,3:T(4,128)S(1)} %get-tuple-element.32), channel_id=1, source_target_pairs={{0,1},{1,0},{2,3},{3,2},{4,5},{5,4},{6,7},{7,6},{8,9},{9,8},{10,11... | collective-permute-start | bytes 73736 | tf_op jit(solution)/shard_map/ppermute | solution.py:42
  21.6 7.3 %collective-permute-start.8 = (f32[4,3,4,1,128]{4,2,1,0,3:T(4,128)S(1)}, f32[4,3,4,1,128]{4,2,1,0,3:T(4,128)S(1)}, u32[]{:S(2)}, u32[]{:S(2)}) collective-permute-start(f32[4,3,4,1,128]{4,2,1,0,3:T(4,128)S(1)} %get-tuple-element.33), channel_id=1, source_target_pairs={{0,16},{1,2},{2,1},{3,19},{16,0},{17,18},{18,17},{19,3},{4,20},{5,... | collective-permute-start | bytes 73736 | tf_op jit(solution)/shard_map/ppermute | solution.py:42

commit v3 on v2

--- a/solution.py
+++ b/solution.py
@@ -363,8 +363,15 @@
         else:
             lax.fori_loop(first, last, cell, 0)
 
-    for used in range(1, limit + 1):
-        pl.when(blocks == used)(functools.partial(with_blocks, used))
+    def choose(low, high):
+        if low == high:
+            with_blocks(low)
+            return
+        middle = (low + high) // 2
+        pl.when(blocks <= middle)(functools.partial(choose, low, middle))
+        pl.when(blocks > middle)(functools.partial(choose, middle + 1, high))
+
+    pl.when(blocks > 0)(functools.partial(choose, 1, limit))
 
 
 def repeat(rows, out, slots):

time: 31.7 us -> 31.5 us (level)
  no operation moved by 1% of the time
where the time goes in v3:
time: 31.5 us; the launch traced here: 31.1 us
  Pallas kernels  12.8 us (41%)
  waiting for transfers between devices  9.12 us (29%)
  starting transfers between devices  8.09 us (26%)
  between operations  0.84 us (3%)
    pallas_call x10, Pallas kernels, call(): pl.pallas_call(kernel, out_shape=[jax.ShapeDtypeStruct(shape, dtype) for...  12.8 us
    ppermute x10, waiting for transfers between devices, swap(): return lax.ppermute(message, names, pairs)  9.12 us
    ppermute x10, starting transfers between devices, swap(): return lax.ppermute(message, names, pairs)  8.09 us
  transfers between devices with their start and end apart: 10, of which 6 were waited for; matrix products, arithmetic and copies ran while one was open for 0% of the time, Pallas kernels for 29%

profile of v3, /device:TPU:12, one launch (start us, length us, event | category | flops | bytes accessed | tf_op | source)
XLA Modules:
  0.0 31.1 jit_solution(17121869252458187746)
XLA Ops:
  0.6 0.9 %shard_map.59 = (f32[32,128]{1,0:T(8,128)S(1)}, f32[24,128]{1,0:T(8,128)S(1)}) custom-call(s32[2,2,2]{2,1,0:T(2,128)} %refs_0_.1, f32[8,128]{1,0:T(8,128)} %bitcast.25, f32[24,128]{1,0:T(8,128)} %bitcast.23, f32[24,128]{1,0:T(8,128)} %bitcast.24), custom_call_target="tpu_custom_call" | custom-call | flops 1048576 | bytes 1048576 | tf_op jit(solution)/shard_map/pallas_call | solution.py:470
  1.7 1.1 %collective-permute-done = f32[4,1,2,2,128]{4,2,1,0,3:T(2,128)S(1)} collective-permute-done((f32[4,1,2,2,128]{4,2,1,0,3:T(2,128)S(1)}, f32[4,1,2,2,128]{4,2,1,0,3:T(2,128)S(1)}, u32[]{:S(2)}, u32[]{:S(2)}) %collective-permute-start) | collective-permute-done | bytes 8224 | tf_op jit(solution)/shard_map/ppermute | solution.py:42
  2.9 1.6 %collective-permute-start.1 = (f32[4,3,1,2,128]{4,2,1,0,3:T(1,128)S(1)}, f32[4,3,1,2,128]{4,2,1,0,3:T(1,128)S(1)}, u32[]{:S(2)}, u32[]{:S(2)}) collective-permute-start(f32[4,3,1,2,128]{4,2,1,0,3:T(1,128)S(1)} %get-tuple-element.38), channel_id=1, source_target_pairs={{0,4},{4,0},{8,12},{12,8},{1,5},{5,1},{9,13},{13,9},{2,6},{6,2},{1... | collective-permute-start | bytes 36872 | tf_op jit(solution)/shard_map/ppermute | solution.py:42
  4.4 0.5 %collective-permute-start.2 = (f32[4,3,1,2,128]{4,2,1,0,3:T(1,128)S(1)}, f32[4,3,1,2,128]{4,2,1,0,3:T(1,128)S(1)}, u32[]{:S(2)}, u32[]{:S(2)}) collective-permute-start(f32[4,3,1,2,128]{4,2,1,0,3:T(1,128)S(1)} %get-tuple-element.39), channel_id=1, source_target_pairs={{0,16},{4,8},{8,4},{12,28},{16,0},{20,24},{24,20},{28,12},{1,17},{... | collective-permute-start | bytes 36872 | tf_op jit(solution)/shard_map/ppermute | solution.py:42
  4.9 1.7 %collective-permute-done.1 = f32[4,3,1,2,128]{4,2,1,0,3:T(1,128)S(1)} collective-permute-done((f32[4,3,1,2,128]{4,2,1,0,3:T(1,128)S(1)}, f32[4,3,1,2,128]{4,2,1,0,3:T(1,128)S(1)}, u32[]{:S(2)}, u32[]{:S(2)}) %collective-permute-start.1) | collective-permute-done | bytes 12320 | tf_op jit(solution)/shard_map/ppermute | solution.py:42
  6.6 2.4 %collective-permute-done.2 = f32[4,3,1,2,128]{4,2,1,0,3:T(1,128)S(1)} collective-permute-done((f32[4,3,1,2,128]{4,2,1,0,3:T(1,128)S(1)}, f32[4,3,1,2,128]{4,2,1,0,3:T(1,128)S(1)}, u32[]{:S(2)}, u32[]{:S(2)}) %collective-permute-start.2) | collective-permute-done | bytes 12320 | tf_op jit(solution)/shard_map/ppermute | solution.py:42
  9.1 0.5 %collective-permute-start.4 = (f32[4,3,4,1,128]{4,2,1,0,3:T(4,128)S(1)}, f32[4,3,4,1,128]{4,2,1,0,3:T(4,128)S(1)}, u32[]{:S(2)}, u32[]{:S(2)}) collective-permute-start(f32[4,3,4,1,128]{4,2,1,0,3:T(4,128)S(1)} %get-tuple-element.34), channel_id=1, source_target_pairs={{0,1},{1,0},{2,3},{3,2},{4,5},{5,4},{6,7},{7,6},{8,9},{9,8},{10,11... | collective-permute-start | bytes 73736 | tf_op jit(solution)/shard_map/ppermute | solution.py:42
  9.6 2.7 %collective-permute-start.3 = (f32[4,3,4,1,128]{4,2,1,0,3:T(4,128)S(1)}, f32[4,3,4,1,128]{4,2,1,0,3:T(4,128)S(1)}, u32[]{:S(2)}, u32[]{:S(2)}) collective-permute-start(f32[4,3,4,1,128]{4,2,1,0,3:T(4,128)S(1)} %get-tuple-element.35), channel_id=1, source_target_pairs={{0,16},{1,2},{2,1},{3,19},{16,0},{17,18},{18,17},{19,3},{4,20},{5,... | collective-permute-start | bytes 73736 | tf_op jit(solution)/shard_map/ppermute | solution.py:42
  12.3 1.8 %shard_map.60 = (f32[96,128]{1,0:T(8,128)S(1)}, bf16[4,32,256]{2,1,0:T(8,128)(2,1)S(1)}, f32[4,8,256]{2,1,0:T(8,128)S(1)}) custom-call(f32[96,128]{1,0:T(8,128)S(1)} %bitcast.18), custom_call_target="tpu_custom_call" | custom-call | flops 134217728 | bytes 1048576 | tf_op jit(solution)/shard_map/pallas_call | solution.py:470
  14.1 0.6 %shard_map.61 = (f32[48,128]{1,0:T(8,128)S(1)}, f32[4,8,256]{2,1,0:T(8,128)S(1)}) custom-call(f32[48,128]{1,0:T(8,128)S(1)} %bitcast.22, bf16[4,32,256]{2,1,0:T(8,128)(2,1)S(1)} %get-tuple-element.19.right, f32[4,8,256]{2,1,0:T(8,128)S(1)} %get-tuple-element.20.sums), custom_call_target="tpu_custom_call" | custom-call | flops 33554432 | bytes 1048576 | tf_op jit(solution)/shard_map/pallas_call | solution.py:470
  14.8 0.7 %shard_map.62 = (f32[48,128]{1,0:T(8,128)S(1)}, f32[32,128]{1,0:T(8,128)S(1)}, f32[8,128]{1,0:T(8,128)S(1)}) custom-call(f32[48,128]{1,0:T(8,128)S(1)} %bitcast.21, f32[32,128]{1,0:T(8,128)S(1)} %get-tuple-element.17.state.cells, f32[24,128]{1,0:T(8,128)S(1)} %get-tuple-element.18.speed, bf16[4,32,256]{2,1,0:T(8,128)(2,1)S(1)} %get-tuple-element.19.right, ...), custom_call_target="tpu_custom_call" | custom-call | flops 33554432 | bytes 1048576 | tf_op jit(solution)/shard_map/pallas_call | solution.py:470
  15.4 0.1 collective-permute-start.5
  15.5 1.1 %collective-permute-done.5 = f32[4,1,2,2,128]{4,2,1,0,3:T(2,128)S(1)} collective-permute-done((f32[4,1,2,2,128]{4,2,1,0,3:T(2,128)S(1)}, f32[4,1,2,2,128]{4,2,1,0,3:T(2,128)S(1)}, u32[]{:S(2)}, u32[]{:S(2)}) %collective-permute-start.5) | collective-permute-done | bytes 8224 | tf_op jit(solution)/shard_map/ppermute | solution.py:42
  16.8 0.5 %collective-permute-start.7 = (f32[4,3,1,2,128]{4,2,1,0,3:T(1,128)S(1)}, f32[4,3,1,2,128]{4,2,1,0,3:T(1,128)S(1)}, u32[]{:S(2)}, u32[]{:S(2)}) collective-permute-start(f32[4,3,1,2,128]{4,2,1,0,3:T(1,128)S(1)} %get-tuple-element.37), channel_id=1, source_target_pairs={{0,16},{4,8},{8,4},{12,28},{16,0},{20,24},{24,20},{28,12},{1,17},{... | collective-permute-start | bytes 36872 | tf_op jit(solution)/shard_map/ppermute | solution.py:42
  17.3 0.6 %shard_map.63.columns = f32[3,8,128,128]{3,2,1,0:T(8,128)S(1)} custom-call(f32[32,128]{1,0:T(8,128)S(1)} %get-tuple-element.17.state.cells), custom_call_target="tpu_custom_call" | custom-call | flops 67108864 | bytes 1048576 | tf_op jit(solution)/shard_map/pallas_call | solution.py:470
  17.9 0.8 %shard_map.64 = (f32[8,128,128]{2,1,0:T(8,128)S(1)}, f32[8,128]{1,0:T(8,128)}) custom-call(f32[32,128]{1,0:T(8,128)S(1)} %get-tuple-element.22.flow.own, f32[8,128]{1,0:T(8,128)S(1)} %get-tuple-element.24.density), custom_call_target="tpu_custom_call" | custom-call | flops 33554432 | bytes 1048576 | tf_op jit(solution)/shard_map/pallas_call | solution.py:470
  18.7 1.7 %collective-permute-done.6 = f32[4,3,1,2,128]{4,2,1,0,3:T(1,128)S(1)} collective-permute-done((f32[4,3,1,2,128]{4,2,1,0,3:T(1,128)S(1)}, f32[4,3,1,2,128]{4,2,1,0,3:T(1,128)S(1)}, u32[]{:S(2)}, u32[]{:S(2)}) %collective-permute-start.6) | collective-permute-done | bytes 12320 | tf_op jit(solution)/shard_map/ppermute | solution.py:42
  20.5 1.0 %collective-permute-done.7 = f32[4,3,1,2,128]{4,2,1,0,3:T(1,128)S(1)} collective-permute-done((f32[4,3,1,2,128]{4,2,1,0,3:T(1,128)S(1)}, f32[4,3,1,2,128]{4,2,1,0,3:T(1,128)S(1)}, u32[]{:S(2)}, u32[]{:S(2)}) %collective-permute-start.7) | collective-permute-done | bytes 12320 | tf_op jit(solution)/shard_map/ppermute | solution.py:42
  21.5 0.1 collective-permute-start.9
  21.6 2.0 %collective-permute-start.8 = (f32[4,3,4,1,128]{4,2,1,0,3:T(4,128)S(1)}, f32[4,3,4,1,128]{4,2,1,0,3:T(4,128)S(1)}, u32[]{:S(2)}, u32[]{:S(2)}) collective-permute-start(f32[4,3,4,1,128]{4,2,1,0,3:T(4,128)S(1)} %get-tuple-element.33), channel_id=1, source_target_pairs={{0,16},{1,2},{2,1},{3,19},{16,0},{17,18},{18,17},{19,3},{4,20},{5,... | collective-permute-start | bytes 73736 | tf_op jit(solution)/shard_map/ppermute | solution.py:42
  23.6 1.6 %shard_map.65.start = f32[4,8,128,128]{3,2,1,0:T(8,128)S(1)} custom-call(f32[32,128]{1,0:T(8,128)S(1)} %get-tuple-element.17.state.cells, f32[32,128]{1,0:T(8,128)S(1)} %get-tuple-element.22.flow.own, f32[3,8,128,128]{3,2,1,0:T(8,128)S(1)} %shard_map.63.columns, f32[8,128,128]{2,1,0:T(8,128)S(1)} %get-tuple-element.25.press), custom_call_target="tpu_custom_call" | custom-call | flops 134217728 | bytes 1048576 | tf_op jit(solution)/shard_map/pallas_call | solution.py:470
  25.2 2.0 %shard_map.66.start = f32[4,8,128,128]{3,2,1,0:T(8,128)S(1)} custom-call(f32[32,128]{1,0:T(8,128)S(1)} %get-tuple-element.17.state.cells, f32[96,128]{1,0:T(8,128)S(1)} %get-tuple-element.27.cells, f32[96,128]{1,0:T(8,128)S(1)} %bitcast.17, f32[3,8,128,128]{3,2,1,0:T(8,128)S(1)} %shard_map.63.columns, ...), custom_call_target="tpu_custom_call", output_to_operand_aliasing={{}: (5, {})} | custom-call | flops 134217728 | bytes 1048576 | tf_op jit(solution)/shard_map/pallas_call | solution.py:470
  27.2 1.6 %shard_map.67 = (f32[4,8,128,128]{3,2,1,0:T(8,128)S(1)}, f32[128,128]{1,0:T(8,128)S(1)}) custom-call(f32[32,128]{1,0:T(8,128)S(1)} %get-tuple-element.17.state.cells, f32[48,128]{1,0:T(8,128)S(1)} %get-tuple-element.26.near, f32[48,128]{1,0:T(8,128)S(1)} %bitcast.20, f32[3,8,128,128]{3,2,1,0:T(8,128)S(1)} %shard_map.63.columns, ...), custom_call_target="tpu_custom_call", output_to_operand_aliasing={{0}: (5, {})} | custom-call | flops 67108864 | bytes 1048576 | tf_op jit(solution)/shard_map/pallas_call | solution.py:470
  28.8 2.3 %shard_map.68 = (f32[4,8,128,128]{3,2,1,0:T(8,128)S(1)}, f32[24,128]{1,0:T(8,128)}) custom-call(f32[32,128]{1,0:T(8,128)S(1)} %get-tuple-element.17.state.cells, f32[32,128]{1,0:T(8,128)S(1)} %get-tuple-element.22.flow.own, f32[48,128]{1,0:T(8,128)S(1)} %get-tuple-element.23.near, f32[48,128]{1,0:T(8,128)S(1)} %bitcast.19, ...), custom_call_target="tpu_custom_call", output_to_operand_aliasing={{0}: (6, {})} | custom-call | flops 67108864 | bytes 1048576 | tf_op jit(solution)/shard_map/pallas_call | solution.py:470
  (22 shorter events, 0.4 us)
Async XLA Ops:
  1.6 1.2 %collective-permute-start = (f32[4,1,2,2,128]{4,2,1,0,3:T(2,128)S(1)}, f32[4,1,2,2,128]{4,2,1,0,3:T(2,128)S(1)}, u32[]{:S(2)}, u32[]{:S(2)}) collective-permute-start(f32[4,1,2,2,128]{4,2,1,0,3:T(2,128)S(1)} %copy.17), channel_id=1, source_target_pairs={{0,16},{16,0},{1,17},{17,1},{2,18},{18,2},{3,19},{19,3},{4,20},{20... | collective-permute-start | bytes 24584 | tf_op jit(solution)/shard_map/ppermute | solution.py:42
  2.9 3.8 %collective-permute-start.1 = (f32[4,3,1,2,128]{4,2,1,0,3:T(1,128)S(1)}, f32[4,3,1,2,128]{4,2,1,0,3:T(1,128)S(1)}, u32[]{:S(2)}, u32[]{:S(2)}) collective-permute-start(f32[4,3,1,2,128]{4,2,1,0,3:T(1,128)S(1)} %get-tuple-element.38), channel_id=1, source_target_pairs={{0,4},{4,0},{8,12},{12,8},{1,5},{5,1},{9,13},{13,9},{2,6},{6,2},{1... | collective-permute-start | bytes 36872 | tf_op jit(solution)/shard_map/ppermute | solution.py:42
  4.4 4.6 %collective-permute-start.2 = (f32[4,3,1,2,128]{4,2,1,0,3:T(1,128)S(1)}, f32[4,3,1,2,128]{4,2,1,0,3:T(1,128)S(1)}, u32[]{:S(2)}, u32[]{:S(2)}) collective-permute-start(f32[4,3,1,2,128]{4,2,1,0,3:T(1,128)S(1)} %get-tuple-element.39), channel_id=1, source_target_pairs={{0,16},{4,8},{8,4},{12,28},{16,0},{20,24},{24,20},{28,12},{1,17},{... | collective-permute-start | bytes 36872 | tf_op jit(solution)/shard_map/ppermute | solution.py:42
  9.1 5.0 %collective-permute-start.4 = (f32[4,3,4,1,128]{4,2,1,0,3:T(4,128)S(1)}, f32[4,3,4,1,128]{4,2,1,0,3:T(4,128)S(1)}, u32[]{:S(2)}, u32[]{:S(2)}) collective-permute-start(f32[4,3,4,1,128]{4,2,1,0,3:T(4,128)S(1)} %get-tuple-element.34), channel_id=1, source_target_pairs={{0,1},{1,0},{2,3},{3,2},{4,5},{5,4},{6,7},{7,6},{8,9},{9,8},{10,11... | collective-permute-start | bytes 73736 | tf_op jit(solution)/shard_map/ppermute | solution.py:42
  9.6 5.2 %collective-permute-start.3 = (f32[4,3,4,1,128]{4,2,1,0,3:T(4,128)S(1)}, f32[4,3,4,1,128]{4,2,1,0,3:T(4,128)S(1)}, u32[]{:S(2)}, u32[]{:S(2)}) collective-permute-start(f32[4,3,4,1,128]{4,2,1,0,3:T(4,128)S(1)} %get-tuple-element.35), channel_id=1, source_target_pairs={{0,16},{1,2},{2,1},{3,19},{16,0},{17,18},{18,17},{19,3},{4,20},{5,... | collective-permute-start | bytes 73736 | tf_op jit(solution)/shard_map/ppermute | solution.py:42
  15.4 1.2 %collective-permute-start.5 = (f32[4,1,2,2,128]{4,2,1,0,3:T(2,128)S(1)}, f32[4,1,2,2,128]{4,2,1,0,3:T(2,128)S(1)}, u32[]{:S(2)}, u32[]{:S(2)}) collective-permute-start(f32[4,1,2,2,128]{4,2,1,0,3:T(2,128)S(1)} %copy.18), channel_id=1, source_target_pairs={{0,16},{16,0},{1,17},{17,1},{2,18},{18,2},{3,19},{19,3},{4,20},{20... | collective-permute-start | bytes 24584 | tf_op jit(solution)/shard_map/ppermute | solution.py:42
  16.7 3.8 %collective-permute-start.6 = (f32[4,3,1,2,128]{4,2,1,0,3:T(1,128)S(1)}, f32[4,3,1,2,128]{4,2,1,0,3:T(1,128)S(1)}, u32[]{:S(2)}, u32[]{:S(2)}) collective-permute-start(f32[4,3,1,2,128]{4,2,1,0,3:T(1,128)S(1)} %get-tuple-element.36), channel_id=1, source_target_pairs={{0,4},{4,0},{8,12},{12,8},{1,5},{5,1},{9,13},{13,9},{2,6},{6,2},{1... | collective-permute-start | bytes 36872 | tf_op jit(solution)/shard_map/ppermute | solution.py:42
  16.8 4.7 %collective-permute-start.7 = (f32[4,3,1,2,128]{4,2,1,0,3:T(1,128)S(1)}, f32[4,3,1,2,128]{4,2,1,0,3:T(1,128)S(1)}, u32[]{:S(2)}, u32[]{:S(2)}) collective-permute-start(f32[4,3,1,2,128]{4,2,1,0,3:T(1,128)S(1)} %get-tuple-element.37), channel_id=1, source_target_pairs={{0,16},{4,8},{8,4},{12,28},{16,0},{20,24},{24,20},{28,12},{1,17},{... | collective-permute-start | bytes 36872 | tf_op jit(solution)/shard_map/ppermute | solution.py:42
  21.5 5.7 %collective-permute-start.9 = (f32[4,3,4,1,128]{4,2,1,0,3:T(4,128)S(1)}, f32[4,3,4,1,128]{4,2,1,0,3:T(4,128)S(1)}, u32[]{:S(2)}, u32[]{:S(2)}) collective-permute-start(f32[4,3,4,1,128]{4,2,1,0,3:T(4,128)S(1)} %get-tuple-element.32), channel_id=1, source_target_pairs={{0,1},{1,0},{2,3},{3,2},{4,5},{5,4},{6,7},{7,6},{8,9},{9,8},{10,11... | collective-permute-start | bytes 73736 | tf_op jit(solution)/shard_map/ppermute | solution.py:42
  21.6 7.2 %collective-permute-start.8 = (f32[4,3,4,1,128]{4,2,1,0,3:T(4,128)S(1)}, f32[4,3,4,1,128]{4,2,1,0,3:T(4,128)S(1)}, u32[]{:S(2)}, u32[]{:S(2)}) collective-permute-start(f32[4,3,4,1,128]{4,2,1,0,3:T(4,128)S(1)} %get-tuple-element.33), channel_id=1, source_target_pairs={{0,16},{1,2},{2,1},{3,19},{16,0},{17,18},{18,17},{19,3},{4,20},{5,... | collective-permute-start | bytes 73736 | tf_op jit(solution)/shard_map/ppermute | solution.py:42
